TPU v7x, 32 devices: a whole 2x2x4 slice. The times are simulated.
32 devices in a mesh: clip: 4 (over y, x), blk: 8 (over z, core).
Axes of the slice: x: 2, y: 2, z: 4, core: 2. Of those that a mesh axis runs over, the one named last changes fastest.
Arguments:
- frames: bfloat16 [4, 2048, 1024], P('clip', 'blk'), may hold values from -6 to 6
- text_states: bfloat16 [4, 256, 1024], P('clip'), may hold values from -6 to 6
- prompt_lengths: int32 [4], P('clip'), may hold values from 1 to 256, as said below
- cotangent: bfloat16 [4, 2048, 1024], P('clip', 'blk'), may hold values from -6 to 6
- self_query: bfloat16 [1024, 1024], replicated, may hold values from -0.1875 to 0.1875
- self_key: bfloat16 [1024, 1024], replicated, may hold values from -0.1875 to 0.1875
- self_value: bfloat16 [1024, 1024], replicated, may hold values from -0.1875 to 0.1875
- self_out: bfloat16 [1024, 1024], replicated, may hold values from -1 to 1
- cross_query: bfloat16 [1024, 1024], replicated, may hold values from -0.1875 to 0.1875
- cross_key: bfloat16 [1024, 1024], replicated, may hold values from -0.1875 to 0.1875
- cross_value: bfloat16 [1024, 1024], replicated, may hold values from -0.1875 to 0.1875
- cross_out: bfloat16 [1024, 1024], replicated, may hold values from -0.75 to 0.75
- hidden_in: bfloat16 [1024, 4096], replicated, may hold values from -0.1875 to 0.1875
- hidden_out: bfloat16 [4096, 1024], replicated, may hold values from -0.09375 to 0.09375
- first_gain: float32 [1024], replicated, may hold values from 0.25 to 1.75
- first_shift: float32 [1024], replicated, may hold values from -3 to 3
- second_gain: float32 [1024], replicated, may hold values from 0.25 to 1.75
- second_shift: float32 [1024], replicated, may hold values from -3 to 3
- third_gain: float32 [1024], replicated, may hold values from 0.25 to 1.75
- third_shift: float32 [1024], replicated, may hold values from -3 to 3
Outputs:
- output_frames: bfloat16 [4, 2048, 1024], P('clip', 'blk')
- frames_grad: float32 [4, 2048, 1024], P('clip', 'blk')
- text_grad: float32 [4, 256, 1024], P('clip', 'blk')
- self_query_grad: float32 [1024, 1024], P(('clip', 'blk'))
- self_key_grad: float32 [1024, 1024], P(('clip', 'blk'))
- self_value_grad: float32 [1024, 1024], P(('clip', 'blk'))
- self_out_grad: float32 [1024, 1024], P(('clip', 'blk'))
- cross_query_grad: float32 [1024, 1024], P(('clip', 'blk'))
- cross_key_grad: float32 [1024, 1024], P(('clip', 'blk'))
- cross_value_grad: float32 [1024, 1024], P(('clip', 'blk'))
- cross_out_grad: float32 [1024, 1024], P(('clip', 'blk'))
- hidden_in_grad: float32 [1024, 4096], P(('clip', 'blk'))
- hidden_out_grad: float32 [4096, 1024], P(('clip', 'blk'))
- first_gain_grad: float32 [1024], P(('clip', 'blk'))
- first_shift_grad: float32 [1024], P(('clip', 'blk'))
- second_gain_grad: float32 [1024], P(('clip', 'blk'))
- second_shift_grad: float32 [1024], P(('clip', 'blk'))
- third_gain_grad: float32 [1024], P(('clip', 'blk'))
- third_shift_grad: float32 [1024], P(('clip', 'blk'))
Inputs may be any that keep to these rules, and one draw needn't show every extreme that they name: Each clip's prompt fills its first prompt_lengths tokens of the 256 padded ones. In every draw one clip's prompt fills all 256; the others are at most 64.
All inputs are finite; a program needn't handle non-finite values.
Results may differ from a plain program's by a relative error of at most 0.025.
Values may be sent and summed in bfloat16 or wider, within the bound.
A program may use at most 256 MiB of HBM per device.

v0:
```python
from functools import partial
import math

import jax
import jax.numpy as jnp
from jax import lax
from jax.sharding import PartitionSpec as P

D = 1024
HEADS = 16
HEAD = 64
TEXT = 256


def shifted(block, axis, distance):
    devices = range(lax.axis_size(axis))
    route = [((i - distance) % len(devices), i) for i in devices]
    return lax.ppermute(block, axis, route)


def shifted_2(block, axis, distance):
    devices = range(lax.axis_size(axis))
    route = [(i - distance, i) for i in devices if i - distance in devices]
    return lax.ppermute(block, axis, route)


def layer_norm(inputs, gain_vec, shift_vec):
    centred = inputs - jnp.mean(inputs, axis=-1, keepdims=True)
    variance = jnp.mean(centred * centred, axis=-1, keepdims=True)
    return centred * lax.rsqrt(variance + 1e-05) * gain_vec + shift_vec


def project(left, right):
    return jnp.dot(left, right, preferred_element_type=jnp.float32)


def weight_term(left, right):
    return jnp.einsum("td,te->de", left, right, preferred_element_type=jnp.float32)


def back_project(left, right):
    return jnp.einsum("te,de->td", left, right, preferred_element_type=jnp.float32)


def body(
    frames,
    text_states,
    prompt_lengths,
    cotangent,
    self_query,
    self_key,
    self_value,
    self_out,
    cross_query,
    cross_key,
    cross_value,
    cross_out,
    hidden_in,
    hidden_out,
    first_gain,
    first_shift,
    second_gain,
    second_shift,
    third_gain,
    third_shift,
):
    block_total = lax.axis_size("blk")
    block_rank = lax.axis_index("blk")
    local_frames = frames[0].astype(jnp.float32)
    row_count = local_frames.shape[0]
    normed_one, norm_back_one = jax.vjp(layer_norm, local_frames, first_gain, first_shift)
    act_one = normed_one.astype(jnp.bfloat16)
    queries = project(act_one, self_query).astype(jnp.bfloat16)
    keys_local = project(act_one, self_key).astype(jnp.bfloat16)
    values_local = project(act_one, self_value).astype(jnp.bfloat16)
    query_heads = queries.reshape(row_count, HEADS, HEAD)
    query_index = block_rank * row_count + jnp.arange(row_count, dtype=jnp.int32)
    query_limit = (block_rank + 1) * row_count
    start_state = (
        jnp.full((HEADS, row_count), -1e30, jnp.float32),
        jnp.zeros((HEADS, row_count), jnp.float32),
        jnp.zeros((HEADS, row_count, HEAD), jnp.float32),
    )
    piece_keys = lax.all_gather(keys_local, "blk", axis=0, tiled=True)
    piece_values = lax.all_gather(values_local, "blk", axis=0, tiled=True)
    step_rows = math.gcd(row_count, piece_keys.shape[0])

    def one_step(step_index, running):
        first_key = step_index * step_rows

        def attend(running_in):
            run_peak, run_total, weighted = running_in
            key_block = lax.dynamic_slice_in_dim(piece_keys, step_index * step_rows, step_rows, 0)
            value_block = lax.dynamic_slice_in_dim(
                piece_values, step_index * step_rows, step_rows, 0
            )
            key_block = key_block.reshape(step_rows, HEADS, HEAD)
            value_block = value_block.reshape(step_rows, HEADS, HEAD)
            scores = (
                jnp.einsum(
                    "qhd,khd->hqk", query_heads, key_block, preferred_element_type=jnp.float32
                )
                * 0.125
            )
            key_index = first_key + jnp.arange(step_rows, dtype=jnp.int32)
            allowed = (key_index[None, :] <= query_index[:, None])[None]
            scores = jnp.where(allowed, scores, -1e30)
            new_peak = jnp.maximum(run_peak, jnp.max(scores, axis=-1))
            weights = jnp.where(allowed, jnp.exp(scores - new_peak[..., None]), 0.0)
            rescale = jnp.exp(run_peak - new_peak)
            run_total = run_total * rescale + jnp.sum(weights, axis=-1)
            weighted = weighted * rescale[..., None] + jnp.einsum(
                "hqk,khd->hqd",
                weights.astype(jnp.bfloat16),
                value_block,
                preferred_element_type=jnp.float32,
            )
            return (new_peak, run_total, weighted)

        return lax.cond(first_key < query_limit, attend, lambda running_in: running_in, running)

    run_peak, run_total, weighted = lax.fori_loop(
        0, piece_keys.shape[0] // step_rows, one_step, start_state
    )
    attended = (weighted / run_total[..., None]).transpose(1, 0, 2).reshape(row_count, D)
    log_sum = run_peak + jnp.log(run_total)
    att_low = attended.astype(jnp.bfloat16)
    after_self = local_frames + project(att_low, self_out)
    normed_two, norm_back_two = jax.vjp(layer_norm, after_self, second_gain, second_shift)
    act_two = normed_two.astype(jnp.bfloat16)
    local_text = text_states[0]
    cross_queries = (
        project(act_two, cross_query).astype(jnp.bfloat16).reshape(row_count, HEADS, HEAD)
    )
    text_keys = project(local_text, cross_key).astype(jnp.bfloat16).reshape(TEXT, HEADS, HEAD)
    text_values = project(local_text, cross_value).astype(jnp.bfloat16).reshape(TEXT, HEADS, HEAD)
    visible = (jnp.arange(TEXT, dtype=jnp.int32) < prompt_lengths[0])[None, None, :]
    cross_scores = (
        jnp.einsum("qhd,khd->hqk", cross_queries, text_keys, preferred_element_type=jnp.float32)
        * 0.125
    )
    cross_scores = jnp.where(visible, cross_scores, -1e30)
    cross_exp = jnp.exp(cross_scores - jnp.max(cross_scores, axis=-1, keepdims=True))
    cross_prob = cross_exp / jnp.sum(cross_exp, axis=-1, keepdims=True)
    cross_low = cross_prob.astype(jnp.bfloat16)
    cross_mixed = (
        jnp.einsum("hqk,khd->qhd", cross_low, text_values, preferred_element_type=jnp.float32)
        .reshape(row_count, D)
        .astype(jnp.bfloat16)
    )
    after_cross = after_self + project(cross_mixed, cross_out)
    normed_three, norm_back_three = jax.vjp(layer_norm, after_cross, third_gain, third_shift)
    act_three = normed_three.astype(jnp.bfloat16)
    pre_act = project(act_three, hidden_in)
    hidden, gelu_back = jax.vjp(partial(jax.nn.gelu, approximate=False), pre_act)
    hidden_low = hidden.astype(jnp.bfloat16)
    output_frames = (after_cross + project(hidden_low, hidden_out)).astype(jnp.bfloat16)[None]
    grad_out = cotangent[0]
    hidden_out_term = weight_term(hidden_low, grad_out)
    (pre_grad,) = gelu_back(back_project(grad_out, hidden_out))
    pre_low = pre_grad.astype(jnp.bfloat16)
    hidden_in_term = weight_term(act_three, pre_low)
    grad_norm_three, third_gain_term, third_shift_term = norm_back_three(
        back_project(pre_low, hidden_in)
    )
    grad_two = grad_out.astype(jnp.float32) + grad_norm_three
    grad_two_low = grad_two.astype(jnp.bfloat16)
    cross_out_term = weight_term(cross_mixed, grad_two_low)
    mixed_grad = (
        back_project(grad_two_low, cross_out).astype(jnp.bfloat16).reshape(row_count, HEADS, HEAD)
    )
    cross_dprob = jnp.einsum(
        "qhd,khd->hqk", mixed_grad, text_values, preferred_element_type=jnp.float32
    )
    cross_dscore = cross_prob * (
        cross_dprob - jnp.sum(cross_prob * cross_dprob, axis=-1, keepdims=True)
    )
    cross_dscore = cross_dscore.astype(jnp.bfloat16)
    cq_grad = (
        (
            jnp.einsum("hqk,khd->qhd", cross_dscore, text_keys, preferred_element_type=jnp.float32)
            * 0.125
        )
        .reshape(row_count, D)
        .astype(jnp.bfloat16)
    )
    key_part = (
        jnp.einsum(
            "hqk,qhd->khd", cross_dscore, cross_queries, preferred_element_type=jnp.float32
        ).reshape(TEXT, D)
        * 0.125
    )
    value_part = jnp.einsum(
        "hqk,qhd->khd", cross_low, mixed_grad, preferred_element_type=jnp.float32
    ).reshape(TEXT, D)
    key_summed, value_summed = (
        lax.psum_scatter(
            key_part.astype(jnp.bfloat16), "blk", scatter_dimension=0, tiled=True
        ).astype(jnp.float32),
        lax.psum_scatter(
            value_part.astype(jnp.bfloat16), "blk", scatter_dimension=0, tiled=True
        ).astype(jnp.float32),
    )
    text_rows = key_summed.shape[0]
    key_summed_low = key_summed.astype(jnp.bfloat16)
    value_summed_low = value_summed.astype(jnp.bfloat16)
    own_text = lax.dynamic_slice_in_dim(local_text, block_rank * text_rows, text_rows, 0)
    cross_key_term = weight_term(own_text, key_summed_low)
    cross_value_term = weight_term(own_text, value_summed_low)
    text_grad = (
        back_project(key_summed_low, cross_key) + back_project(value_summed_low, cross_value)
    )[None]
    cross_query_term = weight_term(act_two, cq_grad)
    grad_norm_two, second_gain_term, second_shift_term = norm_back_two(
        back_project(cq_grad, cross_query)
    )
    grad_one = grad_two + grad_norm_two
    grad_one_low = grad_one.astype(jnp.bfloat16)
    self_out_term = weight_term(att_low, grad_one_low)
    att_grad = back_project(grad_one_low, self_out).astype(jnp.bfloat16)
    grad_heads = att_grad.reshape(row_count, HEADS, HEAD)
    delta_rows = jnp.sum(
        (att_grad.astype(jnp.float32) * attended).reshape(row_count, HEADS, HEAD), axis=-1
    ).T

    def block_terms(held_keys, held_values, source_block):
        key_block = held_keys.reshape(row_count, HEADS, HEAD)
        value_block = held_values.reshape(row_count, HEADS, HEAD)
        key_index = source_block * row_count + jnp.arange(row_count, dtype=jnp.int32)
        allowed = (key_index[None, :] <= query_index[:, None])[None]
        scores = (
            jnp.einsum("qhd,khd->hqk", query_heads, key_block, preferred_element_type=jnp.float32)
            * 0.125
        )
        scores = jnp.where(allowed, scores, -1e30)
        probs = jnp.where(allowed, jnp.exp(scores - log_sum[..., None]), 0.0)
        dprobs = jnp.einsum(
            "qhd,khd->hqk", grad_heads, value_block, preferred_element_type=jnp.float32
        )
        dscores = (probs * (dprobs - delta_rows[..., None])).astype(jnp.bfloat16)
        query_term = (
            jnp.einsum("hqk,khd->hqd", dscores, key_block, preferred_element_type=jnp.float32)
            * 0.125
        )
        key_term = (
            jnp.einsum(
                "hqk,qhd->khd", dscores, query_heads, preferred_element_type=jnp.float32
            ).reshape(row_count, D)
            * 0.125
        )
        value_term = jnp.einsum(
            "hqk,qhd->khd",
            probs.astype(jnp.bfloat16),
            grad_heads,
            preferred_element_type=jnp.float32,
        ).reshape(row_count, D)
        return (key_term, value_term, query_term)

    def block_grads(held_state, source_block):

        def compute(state_in):
            held_keys, held_values, key_grads, value_grads, query_grads = state_in
            key_term, value_term, query_term = block_terms(held_keys, held_values, source_block)
            return (
                held_keys,
                held_values,
                key_grads + key_term,
                value_grads + value_term,
                query_grads + query_term,
            )

        return lax.cond(source_block <= block_rank, compute, lambda state_in: state_in, held_state)

    def pass_grads(held_state):
        held_keys, held_values, key_grads, value_grads, query_grads = held_state
        key_grads, value_grads = (
            shifted(key_grads.astype(jnp.bfloat16), "blk", 1).astype(key_grads.dtype),
            shifted(value_grads.astype(jnp.bfloat16), "blk", 1).astype(value_grads.dtype),
        )
        return (held_keys, held_values, key_grads, value_grads, query_grads)

    def block_turn(turn, held_state):
        held_state = block_grads(held_state, (block_rank - turn) % block_total)
        held_keys, held_values, key_grads, value_grads, query_grads = pass_grads(held_state)
        held_keys, held_values = shifted_2((held_keys, held_values), "blk", 1)
        return (held_keys, held_values, key_grads, value_grads, query_grads)

    held_state = (
        keys_local,
        values_local,
        jnp.zeros((row_count, D), jnp.float32),
        jnp.zeros((row_count, D), jnp.float32),
        jnp.zeros((HEADS, row_count, HEAD), jnp.float32),
    )
    held_state = lax.fori_loop(0, block_total - 1, block_turn, held_state)
    held_state = block_grads(held_state, (block_rank + 1) % block_total)
    held_state = pass_grads(held_state)
    key_grads, value_grads, query_grads = (held_state[2], held_state[3], held_state[4])
    query_low = query_grads.transpose(1, 0, 2).reshape(row_count, D).astype(jnp.bfloat16)
    key_low = key_grads.astype(jnp.bfloat16)
    value_low = value_grads.astype(jnp.bfloat16)
    self_query_term = weight_term(act_one, query_low)
    self_key_term = weight_term(act_one, key_low)
    self_value_term = weight_term(act_one, value_low)
    grad_act_one = (
        back_project(query_low, self_query)
        + back_project(key_low, self_key)
        + back_project(value_low, self_value)
    )
    grad_norm_one, first_gain_term, first_shift_term = norm_back_one(grad_act_one)
    frames_grad = (grad_one + grad_norm_one)[None]
    terms = [
        self_query_term,
        self_key_term,
        self_value_term,
        self_out_term,
        cross_query_term,
        cross_key_term,
        cross_value_term,
        cross_out_term,
        hidden_in_term,
        hidden_out_term,
        first_gain_term,
        first_shift_term,
        second_gain_term,
        second_shift_term,
        third_gain_term,
        third_shift_term,
    ]
    summed = (
        lax.psum_scatter(terms[0], ("clip", "blk"), scatter_dimension=0, tiled=True),
        lax.psum_scatter(terms[1], ("clip", "blk"), scatter_dimension=0, tiled=True),
        lax.psum_scatter(terms[2], ("clip", "blk"), scatter_dimension=0, tiled=True),
        lax.psum_scatter(terms[3], ("clip", "blk"), scatter_dimension=0, tiled=True),
        lax.psum_scatter(terms[4], ("clip", "blk"), scatter_dimension=0, tiled=True),
        lax.psum_scatter(terms[5], ("clip", "blk"), scatter_dimension=0, tiled=True),
        lax.psum_scatter(terms[6], ("clip", "blk"), scatter_dimension=0, tiled=True),
        lax.psum_scatter(terms[7], ("clip", "blk"), scatter_dimension=0, tiled=True),
        lax.psum_scatter(terms[8], ("clip", "blk"), scatter_dimension=0, tiled=True),
        lax.psum_scatter(terms[9], ("clip", "blk"), scatter_dimension=0, tiled=True),
        lax.psum_scatter(terms[10], ("clip", "blk"), scatter_dimension=0, tiled=True),
        lax.psum_scatter(terms[11], ("clip", "blk"), scatter_dimension=0, tiled=True),
        lax.psum_scatter(terms[12], ("clip", "blk"), scatter_dimension=0, tiled=True),
        lax.psum_scatter(terms[13], ("clip", "blk"), scatter_dimension=0, tiled=True),
        lax.psum_scatter(terms[14], ("clip", "blk"), scatter_dimension=0, tiled=True),
        lax.psum_scatter(terms[15], ("clip", "blk"), scatter_dimension=0, tiled=True),
    )
    return (
        output_frames,
        frames_grad,
        text_grad,
        summed[0],
        summed[1],
        summed[2],
        summed[3],
        summed[4],
        summed[5],
        summed[6],
        summed[7],
        summed[8],
        summed[9],
        summed[10],
        summed[11],
        summed[12],
        summed[13],
        summed[14],
        summed[15],
    )


def solution(mesh):
    in_specs = (
        P("clip", "blk", None),
        P("clip", None, None),
        P("clip"),
        P("clip", "blk", None),
        P(),
        P(),
        P(),
        P(),
        P(),
        P(),
        P(),
        P(),
        P(),
        P(),
        P(),
        P(),
        P(),
        P(),
        P(),
        P(),
    )
    out_specs = (
        P("clip", "blk", None),
        P("clip", "blk", None),
        P("clip", "blk", None),
        P(("clip", "blk"), None),
        P(("clip", "blk"), None),
        P(("clip", "blk"), None),
        P(("clip", "blk"), None),
        P(("clip", "blk"), None),
        P(("clip", "blk"), None),
        P(("clip", "blk"), None),
        P(("clip", "blk"), None),
        P(("clip", "blk"), None),
        P(("clip", "blk"), None),
        P(("clip", "blk")),
        P(("clip", "blk")),
        P(("clip", "blk")),
        P(("clip", "blk")),
        P(("clip", "blk")),
        P(("clip", "blk")),
    )
    return jax.shard_map(body, mesh=mesh, in_specs=in_specs, out_specs=out_specs, check_vma=False)
```

profile of v0, /device:TPU:0, one launch (start us, length us, event | category | flops | bytes accessed | tf_op | source)
XLA Modules:
  0.0 1818.7 jit_solution(14084102031819649447)
XLA Ops:
  32.5 30.8 %all-gather.5.cloned.1.call-done = bf16[2048,1024]{1,0:T(8,128)(2,1)} async-done(((bf16[256,1024]{1,0:T(8,128)(2,1)}), bf16[2048,1024]{1,0:T(8,128)(2,1)}) %all-gather.5.cloned.1.call-update) | async-done | bytes 4194320 | tf_op jit(solution)/shard_map/all_gather | solution.py:85
  69.9 41.6 %all-gather.3.cloned.1.call-done = bf16[2048,1024]{1,0:T(8,128)(2,1)} async-done(((bf16[256,1024]{1,0:T(8,128)(2,1)}), bf16[2048,1024]{1,0:T(8,128)(2,1)}) %all-gather.3.cloned.1.call-update) | async-done | bytes 4194320 | tf_op jit(solution)/shard_map/all_gather | solution.py:84
  141.2 15.5 multiply_convert_fusion.3
  228.3 309.6 %while.43 = (s32[]{:T(128)}, bf16[256,1024]{0,1:T(8,128)(2,1)S(1)}, bf16[256,1024]{0,1:T(8,128)(2,1)}, f32[256,1024]{0,1:T(8,128)}, f32[256,1024]{0,1:T(8,128)},...) while((s32[]{:T(128)}, bf16[256,1024]{0,1:T(8,128)(2,1)S(1)}, ...), condition=%wide.region_23.24_spmd.clone, body=%wide.region_20.0_spmd.clone.sunk | while | flops 686621184 | bytes 66837216 | solution.py:295
  266.9 18.8 %collective-permute-done.3 = bf16[256,1024]{0,1:T(8,128)(2,1)S(1)} collective-permute-done((bf16[256,1024]{0,1:T(8,128)(2,1)}, bf16[256,1024]{0,1:T(8,128)(2,1)S(1)}, u32[]{:S(2)}, u32[]{:S(2)}) %collective-permute-start.3) | collective-permute-done | bytes 524320 | tf_op jit(solution)/shard_map/while/body/eval_jaxpr/ppermute | solution.py:18
  363.8 15.4 collective-permute-start.3
  382.7 16.1 collective-permute-start
  410.6 16.8 collective-permute-start.3
  456.2 12.6 collective-permute-start.3
  472.1 13.7 collective-permute-start
  497.7 17.5 collective-permute-start.3
  518.5 12.0 collective-permute-start
  543.6 16.5 collective-permute-start.5
  560.1 14.4 collective-permute-done.5
  578.8 23.5 %collective-permute-done.4 = bf16[256,1024]{0,1:T(8,128)(2,1)S(1)} collective-permute-done((bf16[256,1024]{0,1:T(8,128)(2,1)S(1)}, bf16[256,1024]{0,1:T(8,128)(2,1)S(1)}, u32[]{:S(2)}, u32[]{:S(2)}) %collective-permute-start.4) | collective-permute-done | bytes 524320 | tf_op jit(solution)/shard_map/ppermute | solution.py:18
  647.4 45.8 %all-reduce.6 = (f32[1024]{0:T(1024)S(1)}, f32[1024]{0:T(1024)S(1)}, f32[1024]{0:T(1024)S(1)}, f32[1024]{0:T(1024)S(1)}, f32[1024]{0:T(1024)S(1)}, /*index=5*/f32[1024]{0:T(1024)S(1)}) all-reduce(f32[1024]{0:T(1024)S(1)} %get-tuple-element.764, ...), channel_id=14, replica_groups=mesh['clip'=4,'blk'=8] {'clip','blk'}, use_global_device_ids=true, to_apply=%region_41.42.clone | all-reduce | flops 6144 | bytes 49152
  705.0 20.5 %reduce-scatter.25.cloned.1.call-done = f32[32,1024]{1,0:T(8,128)} async-done(((f32[1024,1024]{1,0:T(8,128)}), f32[32,1024]{1,0:T(8,128)}) %reduce-scatter.25.cloned.1.call-update) | async-done | bytes 131088 | tf_op jit(solution)/shard_map/reduce_scatter | solution.py:335
  725.5 142.9 %reduce-scatter.17.cloned.1.call-done = f32[32,1024]{1,0:T(8,128)} async-done(((f32[1024,1024]{1,0:T(8,128)}), f32[32,1024]{1,0:T(8,128)}) %reduce-scatter.17.cloned.1.call-update) | async-done | bytes 131088 | tf_op jit(solution)/shard_map/reduce_scatter | solution.py:331
  868.4 142.4 %reduce-scatter.21.cloned.1.call-done = f32[32,1024]{1,0:T(8,128)} async-done(((f32[1024,1024]{1,0:T(8,128)}), f32[32,1024]{1,0:T(8,128)}) %reduce-scatter.21.cloned.1.call-update) | async-done | bytes 131088 | tf_op jit(solution)/shard_map/reduce_scatter | solution.py:333
  1010.8 142.1 %reduce-scatter.19.cloned.1.call-done = f32[32,1024]{1,0:T(8,128)} async-done(((f32[1024,1024]{1,0:T(8,128)}), f32[32,1024]{1,0:T(8,128)}) %reduce-scatter.19.cloned.1.call-update) | async-done | bytes 131088 | tf_op jit(solution)/shard_map/reduce_scatter | solution.py:332
  1152.8 142.9 %reduce-scatter.29.cloned.1.call-done = f32[32,1024]{1,0:T(8,128)} async-done(((f32[1024,1024]{1,0:T(8,128)}), f32[32,1024]{1,0:T(8,128)}) %reduce-scatter.29.cloned.1.call-update) | async-done | bytes 131088 | tf_op jit(solution)/shard_map/reduce_scatter | solution.py:337
  1295.8 142.6 %reduce-scatter.27.cloned.1.call-done = f32[32,1024]{1,0:T(8,128)} async-done(((f32[1024,1024]{1,0:T(8,128)}), f32[32,1024]{1,0:T(8,128)}) %reduce-scatter.27.cloned.1.call-update) | async-done | bytes 131088 | tf_op jit(solution)/shard_map/reduce_scatter | solution.py:336
  1438.3 186.4 %reduce-scatter.33.cloned.1.call-done = f32[32,4096]{1,0:T(8,128)} async-done(((f32[1024,4096]{1,0:T(8,128)}), f32[32,4096]{1,0:T(8,128)}) %reduce-scatter.33.cloned.1.call-update) | async-done | bytes 524304 | tf_op jit(solution)/shard_map/reduce_scatter | solution.py:339
  1624.7 187.1 %reduce-scatter.35.cloned.1.call-done = f32[128,1024]{1,0:T(8,128)} async-done(((f32[4096,1024]{1,0:T(8,128)}), f32[128,1024]{1,0:T(8,128)}) %reduce-scatter.35.cloned.1.call-update) | async-done | bytes 524304 | tf_op jit(solution)/shard_map/reduce_scatter | solution.py:340
  (390 shorter events, 402.5 us)
Async XLA Ops:
  7.2 56.1 %all-gather.5.cloned.1.call-start = ((), (), s32[]{:S(2)}) async-start(), calls=%async_computation.13 | async-start | bytes 4718592 | tf_op jit(solution)/shard_map/all_gather | solution.py:85
  13.4 98.1 %all-gather.3.cloned.1.call-start = ((), (), s32[]{:S(2)}) async-start(), calls=%async_computation.12 | async-start | bytes 4718592 | tf_op jit(solution)/shard_map/all_gather | solution.py:84
  16.6 588.7 %reduce-scatter.39.cloned.1.call-start = ((), (), s32[]{:S(2)}) async-start(), calls=%async_computation.25 | async-start | bytes 589824
  187.3 421.7 %reduce-scatter.37.cloned.1.call-start = ((), (), s32[]{:S(2)}) async-start(), calls=%async_computation.24 | async-start | bytes 589824
  196.9 508.1 %reduce-scatter.31.cloned.1.call-start = ((), (), s32[]{:S(2)}) async-start(), calls=%async_computation.21 | async-start | bytes 4325376 | tf_op jit(solution)/shard_map/reduce_scatter | solution.py:338
  201.0 504.1 %reduce-scatter.23.cloned.1.call-start = ((), (), s32[]{:S(2)}) async-start(), calls=%async_computation.17 | async-start | bytes 4325376 | tf_op jit(solution)/shard_map/reduce_scatter | solution.py:334
  210.9 514.6 %reduce-scatter.25.cloned.1.call-start = ((), (), s32[]{:S(2)}) async-start(), calls=%async_computation.18 | async-start | bytes 4325376 | tf_op jit(solution)/shard_map/reduce_scatter | solution.py:335
  215.2 653.2 %reduce-scatter.17.cloned.1.call-start = ((), (), s32[]{:S(2)}) async-start(), calls=%async_computation.14 | async-start | bytes 4325376 | tf_op jit(solution)/shard_map/reduce_scatter | solution.py:331
  237.5 48.3 %collective-permute-start.3 = (bf16[256,1024]{0,1:T(8,128)(2,1)}, bf16[256,1024]{0,1:T(8,128)(2,1)S(1)}, u32[]{:S(2)}, u32[]{:S(2)}) collective-permute-start(bf16[256,1024]{0,1:T(8,128)(2,1)} %convert_element_type.390), channel_id=1, source_target_pairs={{7,0},{0,1},{1,2},{2,3},{3,4},{4,5},{5,6},{6,7},{15,8},{8,9},{9,10... | collective-permute-start | bytes 1572872 | tf_op jit(solution)/shard_map/while/body/eval_jaxpr/ppermute | solution.py:18
  244.1 47.6 %collective-permute-start.2 = (bf16[256,1024]{0,1:T(8,128)(2,1)}, bf16[256,1024]{0,1:T(8,128)(2,1)S(1)}, u32[]{:S(2)}, u32[]{:S(2)}) collective-permute-start(bf16[256,1024]{0,1:T(8,128)(2,1)} %convert_element_type.388), channel_id=1, source_target_pairs={{7,0},{0,1},{1,2},{2,3},{3,4},{4,5},{5,6},{6,7},{15,8},{8,9},{9,10... | collective-permute-start | bytes 1572872 | tf_op jit(solution)/shard_map/while/body/eval_jaxpr/ppermute | solution.py:18
  249.4 43.3 %collective-permute-start = (bf16[256,1024]{0,1:T(8,128)(2,1)S(1)}, bf16[256,1024]{0,1:T(8,128)(2,1)S(1)}, u32[]{:S(2)}, u32[]{:S(2)}) collective-permute-start(bf16[256,1024]{0,1:T(8,128)(2,1)S(1)} %copy.136), channel_id=1, source_target_pairs={{0,1},{1,2},{2,3},{3,4},{4,5},{5,6},{6,7},{8,9},{9,10},{10,11},{11... | collective-permute-start | bytes 1572872 | tf_op jit(solution)/shard_map/while/body/eval_jaxpr/ppermute | solution.py:24
  257.2 35.6 %collective-permute-start.1 = (bf16[256,1024]{0,1:T(8,128)(2,1)}, bf16[256,1024]{0,1:T(8,128)(2,1)}, u32[]{:S(2)}, u32[]{:S(2)}) collective-permute-start(bf16[256,1024]{0,1:T(8,128)(2,1)} %copy.137), channel_id=1, source_target_pairs={{0,1},{1,2},{2,3},{3,4},{4,5},{5,6},{6,7},{8,9},{9,10},{10,11},{11... | collective-permute-start | bytes 1572872 | tf_op jit(solution)/shard_map/while/body/eval_jaxpr/ppermute | solution.py:24
  327.1 30.1 %collective-permute-start.3 = (bf16[256,1024]{0,1:T(8,128)(2,1)}, bf16[256,1024]{0,1:T(8,128)(2,1)S(1)}, u32[]{:S(2)}, u32[]{:S(2)}) collective-permute-start(bf16[256,1024]{0,1:T(8,128)(2,1)} %convert_element_type.390), channel_id=1, source_target_pairs={{7,0},{0,1},{1,2},{2,3},{3,4},{4,5},{5,6},{6,7},{15,8},{8,9},{9,10... | collective-permute-start | bytes 1572872 | tf_op jit(solution)/shard_map/while/body/eval_jaxpr/ppermute | solution.py:18
  363.8 40.2 %collective-permute-start.3 = (bf16[256,1024]{0,1:T(8,128)(2,1)}, bf16[256,1024]{0,1:T(8,128)(2,1)S(1)}, u32[]{:S(2)}, u32[]{:S(2)}) collective-permute-start(bf16[256,1024]{0,1:T(8,128)(2,1)} %convert_element_type.390), channel_id=1, source_target_pairs={{7,0},{0,1},{1,2},{2,3},{3,4},{4,5},{5,6},{6,7},{15,8},{8,9},{9,10... | collective-permute-start | bytes 1572872 | tf_op jit(solution)/shard_map/while/body/eval_jaxpr/ppermute | solution.py:18
  410.6 39.0 %collective-permute-start.3 = (bf16[256,1024]{0,1:T(8,128)(2,1)}, bf16[256,1024]{0,1:T(8,128)(2,1)S(1)}, u32[]{:S(2)}, u32[]{:S(2)}) collective-permute-start(bf16[256,1024]{0,1:T(8,128)(2,1)} %convert_element_type.390), channel_id=1, source_target_pairs={{7,0},{0,1},{1,2},{2,3},{3,4},{4,5},{5,6},{6,7},{15,8},{8,9},{9,10... | collective-permute-start | bytes 1572872 | tf_op jit(solution)/shard_map/while/body/eval_jaxpr/ppermute | solution.py:18
  456.2 34.8 %collective-permute-start.3 = (bf16[256,1024]{0,1:T(8,128)(2,1)}, bf16[256,1024]{0,1:T(8,128)(2,1)S(1)}, u32[]{:S(2)}, u32[]{:S(2)}) collective-permute-start(bf16[256,1024]{0,1:T(8,128)(2,1)} %convert_element_type.390), channel_id=1, source_target_pairs={{7,0},{0,1},{1,2},{2,3},{3,4},{4,5},{5,6},{6,7},{15,8},{8,9},{9,10... | collective-permute-start | bytes 1572872 | tf_op jit(solution)/shard_map/while/body/eval_jaxpr/ppermute | solution.py:18
  497.7 38.1 %collective-permute-start.3 = (bf16[256,1024]{0,1:T(8,128)(2,1)}, bf16[256,1024]{0,1:T(8,128)(2,1)S(1)}, u32[]{:S(2)}, u32[]{:S(2)}) collective-permute-start(bf16[256,1024]{0,1:T(8,128)(2,1)} %convert_element_type.390), channel_id=1, source_target_pairs={{7,0},{0,1},{1,2},{2,3},{3,4},{4,5},{5,6},{6,7},{15,8},{8,9},{9,10... | collective-permute-start | bytes 1572872 | tf_op jit(solution)/shard_map/while/body/eval_jaxpr/ppermute | solution.py:18
  542.3 468.5 %reduce-scatter.21.cloned.1.call-start = ((), (), s32[]{:S(2)}) async-start(), calls=%async_computation.16 | async-start | bytes 4325376 | tf_op jit(solution)/shard_map/reduce_scatter | solution.py:333
  543.6 30.9 %collective-permute-start.5 = (bf16[256,1024]{0,1:T(8,128)(2,1)S(1)}, bf16[256,1024]{0,1:T(8,128)(2,1)S(1)}, u32[]{:S(2)}, u32[]{:S(2)}) collective-permute-start(bf16[256,1024]{0,1:T(8,128)(2,1)S(1)} %convert_element_type.245), channel_id=1, source_target_pairs={{7,0},{0,1},{1,2},{2,3},{3,4},{4,5},{5,6},{6,7},{15,8},{8,9},{9,10... | collective-permute-start | bytes 1572872 | tf_op jit(solution)/shard_map/ppermute | solution.py:18
  577.4 575.4 %reduce-scatter.19.cloned.1.call-start = ((), (), s32[]{:S(2)}) async-start(), calls=%async_computation.15 | async-start | bytes 4325376 | tf_op jit(solution)/shard_map/reduce_scatter | solution.py:332
  605.2 690.5 %reduce-scatter.29.cloned.1.call-start = ((), (), s32[]{:S(2)}) async-start(), calls=%async_computation.20 | async-start | bytes 4325376 | tf_op jit(solution)/shard_map/reduce_scatter | solution.py:337
  608.9 829.4 %reduce-scatter.27.cloned.1.call-start = ((), (), s32[]{:S(2)}) async-start(), calls=%async_computation.19 | async-start | bytes 4325376 | tf_op jit(solution)/shard_map/reduce_scatter | solution.py:336
  612.7 1012.0 %reduce-scatter.33.cloned.1.call-start = ((), (), s32[]{:S(2)}) async-start(), calls=%async_computation.22 | async-start | bytes 17301504 | tf_op jit(solution)/shard_map/reduce_scatter | solution.py:339
  622.6 1189.2 %reduce-scatter.35.cloned.1.call-start = ((), (), s32[]{:S(2)}) async-start(), calls=%async_computation.23 | async-start | bytes 17301504 | tf_op jit(solution)/shard_map/reduce_scatter | solution.py:340
  (79 other events, 1943.3 us)
Sparse Core Ops, SparseCore 0:
  13.5 49.8 all-gather.4
  65.6 45.8 all-gather.2
  187.4 68.3 reduce-scatter.38
  258.0 29.6 reduce-scatter.36
  290.4 145.0 reduce-scatter.30
  438.2 143.7 reduce-scatter.22
  584.8 140.6 reduce-scatter.24
  728.3 140.0 reduce-scatter.16
  871.3 139.4 reduce-scatter.20
  1013.5 139.3 reduce-scatter.18
  1155.7 140.0 reduce-scatter.28
  1298.5 139.8 reduce-scatter.26
  1441.2 183.4 reduce-scatter.32
  1627.4 184.3 reduce-scatter.34
where the time goes:
time: 1830 us; the launch traced here: 1820 us
  waiting for transfers between devices  1250 us (68%)
  starting transfers between devices  235 us (13%)
  matrix products  151 us (8%)
  local copies, waits for them, and re-layouts  65.1 us (4%)
  other arithmetic  53.1 us (3%)
  blocking collectives  45.8 us (3%)
    reduce_scatter x1, waiting for transfers between devices, body(): lax.psum_scatter(terms[9], ('clip', 'blk'), scatter_dimension=0, tiled=True)  187 us
    reduce_scatter x1, waiting for transfers between devices, body(): lax.psum_scatter(terms[8], ('clip', 'blk'), scatter_dimension=0, tiled=True)  186 us
    reduce_scatter x1, waiting for transfers between devices, body(): lax.psum_scatter(terms[0], ('clip', 'blk'), scatter_dimension=0, tiled=True)  143 us
    reduce_scatter x1, waiting for transfers between devices, body(): lax.psum_scatter(terms[6], ('clip', 'blk'), scatter_dimension=0, tiled=True)  143 us
    reduce_scatter x1, waiting for transfers between devices, body(): lax.psum_scatter(terms[5], ('clip', 'blk'), scatter_dimension=0, tiled=True)  143 us
    reduce_scatter x1, waiting for transfers between devices, body(): lax.psum_scatter(terms[2], ('clip', 'blk'), scatter_dimension=0, tiled=True)  142 us
    reduce_scatter x1, waiting for transfers between devices, body(): lax.psum_scatter(terms[1], ('clip', 'blk'), scatter_dimension=0, tiled=True)  142 us
    ppermute x14, starting transfers between devices, shifted_2(): return lax.ppermute(block, axis, route)  121 us
  transfers between devices with their start and end apart: 44, of which 16 were waited for; matrix products, arithmetic and copies ran while one was open for 10% of the time, Pallas kernels for 0%

commit v1 on v0

--- a/solution.py
+++ b/solution.py
@@ -4,12 +4,15 @@
 import jax
 import jax.numpy as jnp
 from jax import lax
+from jax.experimental import pallas as pl
+from jax.experimental.pallas import tpu as pltpu
 from jax.sharding import PartitionSpec as P
 
 D = 1024
 HEADS = 16
 HEAD = 64
 TEXT = 256
+MESH = pl.DeviceIdType.MESH
 
 
 def shifted(block, axis, distance):
@@ -40,6 +43,212 @@
 
 def back_project(left, right):
     return jnp.einsum("te,de->td", left, right, preferred_element_type=jnp.float32)
+
+
+def bits_of(size):
+    return size.bit_length() - 1
+
+
+def stage_orders(clips, blks):
+    clip_bits = [("clip", k) for k in range(bits_of(clips))]
+    blk_bits = [("blk", k) for k in range(bits_of(blks))]
+    return (blk_bits[:1] + clip_bits + blk_bits[1:], blk_bits[:1] + clip_bits[::-1] + blk_bits[1:])
+
+
+def post_of(order, stage, clips, blks):
+    left = [("clip", k) for k in range(bits_of(clips))][::-1] + [("blk", k) for k in range(bits_of(blks))][::-1]
+    for done in order[:stage]:
+        left.remove(done)
+    return 1 << (len(left) - 1 - left.index(order[stage]))
+
+
+class Scatter:
+    def __init__(self, order, clips, blks, source, window, own, recvs, send_sems, recv_sems, own_sem):
+        self.order, self.clips, self.blks = order, clips, blks
+        self.source, self.window, self.own, self.recvs = source, window, own, recvs
+        self.send_sems, self.recv_sems, self.own_sem = send_sems, recv_sems, own_sem
+
+    def parts(self, stage):
+        axis, bit = self.order[stage]
+        me = lax.axis_index(axis)
+        mine = (me // (1 << bit)) % 2
+        partner = me + (1 << bit) * (1 - 2 * mine)
+        post = post_of(self.order, stage, self.clips, self.blks)
+        ref = self.source if stage == 0 else self.recvs[stage - 1]
+        return {axis: partner}, mine, post, ref
+
+    def half(self, stage, which, post, ref):
+        count, rows, width = ref.shape
+        window = self.window if stage == 0 else slice(None)
+        return ref.reshape(count // (2 * post), 2, post, rows, width).at[:, which, :, :, window]
+
+    def copy(self, stage):
+        partner, mine, post, ref = self.parts(stage)
+        out = self.half(stage, 1 - mine, post, ref)
+        into = self.recvs[stage]
+        into = into.reshape(into.shape[0] // post, post, *into.shape[1:])
+        return pltpu.make_async_remote_copy(
+            src_ref=out,
+            dst_ref=into,
+            send_sem=self.send_sems.at[stage],
+            recv_sem=self.recv_sems.at[stage],
+            device_id=partner,
+            device_id_type=MESH,
+        )
+
+    def load(self):
+        _, mine, post, ref = self.parts(0)
+        kept = self.half(0, mine, post, ref)
+        into = self.own.reshape(self.own.shape[0] // post, post, *self.own.shape[1:])
+        return pltpu.make_async_copy(kept, into, self.own_sem)
+
+    def add(self, stage):
+        _, mine, post, ref = self.parts(stage)
+        into = self.recvs[stage]
+        count = into.shape[0]
+
+        def one(i, carry):
+            at = i if stage == 0 else ((i // post) * 2 + mine) * post + i % post
+            base = self.own if stage == 0 else ref
+            into[i] = into[i] + base[at]
+            return carry
+
+        lax.fori_loop(0, count, one, 0)
+
+    def last(self, out):
+        stage = len(self.order) - 1
+        _, mine, _, ref = self.parts(stage)
+        out[...] = self.recvs[stage][0].astype(jnp.float32) + ref[mine].astype(jnp.float32)
+
+
+def scatter_kernel(clips, blks, kinds, *refs):
+    orders = stage_orders(clips, blks)
+    stages = len(orders[0])
+    count = len(kinds)
+    n_kind = max(k for k, _, _ in kinds) + 1
+    arrays = refs[: len(set((k, a) for k, a, _ in kinds))]
+    refs = refs[len(arrays) :]
+    vec, refs = refs[0], refs[1:]
+    outs, refs = refs[: len(arrays)], refs[len(arrays) :]
+    vec_out, refs = refs[0], refs[1:]
+    owns, refs = refs[:n_kind], refs[n_kind:]
+    recvs, refs = refs[: n_kind * stages], refs[n_kind * stages :]
+    vec_in, send_sems, recv_sems, own_sems, vec_send, vec_recv = refs
+
+    barrier = pltpu.get_barrier_semaphore()
+    for axis, bit in orders[0]:
+        me = lax.axis_index(axis)
+        partner = me + (1 << bit) * (1 - 2 * ((me // (1 << bit)) % 2))
+        pl.semaphore_signal(barrier, inc=1, device_id={axis: partner}, device_id_type=MESH)
+    pl.semaphore_wait(barrier, stages)
+
+    pieces, targets = [], []
+    seen = [0] * n_kind
+    slots = [owns[k].shape[0] for k in range(n_kind)]
+    for p, (kind, array, part) in enumerate(kinds):
+        width = recvs[kind * stages].shape[-1]
+        window = pl.ds(part * width, width)
+        slot = seen[kind]
+        seen[kind] += 1
+        pieces.append(
+            Scatter(
+                orders[p % 2], clips, blks,
+                arrays[array], window,
+                owns[kind].at[slot % slots[kind]],
+                [recvs[kind * stages + s].at[slot] for s in range(stages)],
+                send_sems.at[p], recv_sems.at[p], own_sems.at[p],
+            )
+        )
+        targets.append(outs[array].at[:, window])
+
+    def vec_copy(stage):
+        axis, bit = orders[0][stage]
+        me = lax.axis_index(axis)
+        partner = me + (1 << bit) * (1 - 2 * ((me // (1 << bit)) % 2))
+        return pltpu.make_async_remote_copy(
+            src_ref=vec_in.at[0, stage],
+            dst_ref=vec_in.at[1, stage],
+            send_sem=vec_send.at[stage],
+            recv_sem=vec_recv.at[stage],
+            device_id={axis: partner},
+            device_id_type=MESH,
+        )
+
+    vec_in[0, 0] = vec[...]
+    vec_copy(0).start()
+    for piece in pieces:
+        piece.copy(0).start()
+    held = {}
+    for p, (kind, _, _) in enumerate(kinds):
+        ahead = [q for q in range(count) if kinds[q][0] == kind]
+        held[p] = ahead
+    started = set()
+
+    def load_ahead(kind, upto):
+        queue = [q for q in range(count) if kinds[q][0] == kind]
+        for q in queue[:upto]:
+            if q not in started:
+                started.add(q)
+                pieces[q].load().start()
+
+    for kind in range(n_kind):
+        load_ahead(kind, slots[kind])
+    done = [0] * n_kind
+    for stage in range(stages):
+        for p, piece in enumerate(pieces):
+            piece.copy(stage).wait()
+            if stage == 0:
+                piece.load().wait()
+            if stage == stages - 1:
+                piece.last(targets[p])
+                continue
+            piece.add(stage)
+            piece.copy(stage + 1).start()
+            if stage == 0:
+                kind = kinds[p][0]
+                done[kind] += 1
+                load_ahead(kind, slots[kind] + done[kind])
+        vec_copy(stage).wait()
+        summed = vec_in[0, stage] + vec_in[1, stage]
+        if stage == stages - 1:
+            vec_out[...] = summed
+        else:
+            vec_in[0, stage + 1] = summed
+            vec_copy(stage + 1).start()
+
+
+def reduce_scatter(arrays, kinds, vec, clips, blks):
+    orders = stage_orders(clips, blks)
+    stages = len(orders[0])
+    devices = clips * blks
+    count = len(kinds)
+    n_kind = max(k for k, _, _ in kinds) + 1
+    shapes, totals = [None] * n_kind, [0] * n_kind
+    parts_of = {}
+    for kind, array, part in kinds:
+        totals[kind] += 1
+        parts_of[array] = max(parts_of.get(array, 0), part + 1)
+    for kind, array, _ in kinds:
+        shapes[kind] = (arrays[array].shape[1], arrays[array].shape[2] // parts_of[array])
+    any_spec = pl.BlockSpec(memory_space=pltpu.MemorySpace.HBM)
+    vmem = pl.BlockSpec(memory_space=pltpu.VMEM)
+    scratch = [pltpu.VMEM((min(3, totals[k]), devices // 2, *shapes[k]), jnp.bfloat16) for k in range(n_kind)]
+    for k in range(n_kind):
+        for s in range(stages):
+            scratch.append(pltpu.VMEM((totals[k], devices >> (s + 1), *shapes[k]), jnp.bfloat16))
+    dma = pltpu.SemaphoreType.DMA
+    scratch += [
+        pltpu.VMEM((2, stages, *vec.shape), jnp.float32),
+        dma((count, stages)), dma((count, stages)), dma((count,)), dma((stages,)), dma((stages,)),
+    ]
+    return pl.pallas_call(
+        partial(scatter_kernel, clips, blks, kinds),
+        out_shape=[jax.ShapeDtypeStruct(a.shape[1:], jnp.float32) for a in arrays] + [jax.ShapeDtypeStruct(vec.shape, jnp.float32)],
+        in_specs=[any_spec] * len(arrays) + [vmem],
+        out_specs=[vmem] * (len(arrays) + 1),
+        scratch_shapes=scratch,
+        compiler_params=pltpu.CompilerParams(collective_id=0, has_side_effects=True, vmem_limit_bytes=56 << 20),
+    )(*arrays, vec)
 
 
 def body(
@@ -309,42 +518,20 @@
     )
     grad_norm_one, first_gain_term, first_shift_term = norm_back_one(grad_act_one)
     frames_grad = (grad_one + grad_norm_one)[None]
-    terms = [
-        self_query_term,
-        self_key_term,
-        self_value_term,
-        self_out_term,
-        cross_query_term,
-        cross_key_term,
-        cross_value_term,
-        cross_out_term,
-        hidden_in_term,
-        hidden_out_term,
-        first_gain_term,
-        first_shift_term,
-        second_gain_term,
-        second_shift_term,
-        third_gain_term,
-        third_shift_term,
+    clip_total = lax.axis_size("clip")
+    devices = clip_total * block_total
+    matrices = [
+        self_query_term, self_key_term, self_value_term, self_out_term, cross_query_term, cross_key_term, cross_value_term, cross_out_term,
+        hidden_in_term, hidden_out_term,
     ]
-    summed = (
-        lax.psum_scatter(terms[0], ("clip", "blk"), scatter_dimension=0, tiled=True),
-        lax.psum_scatter(terms[1], ("clip", "blk"), scatter_dimension=0, tiled=True),
-        lax.psum_scatter(terms[2], ("clip", "blk"), scatter_dimension=0, tiled=True),
-        lax.psum_scatter(terms[3], ("clip", "blk"), scatter_dimension=0, tiled=True),
-        lax.psum_scatter(terms[4], ("clip", "blk"), scatter_dimension=0, tiled=True),
-        lax.psum_scatter(terms[5], ("clip", "blk"), scatter_dimension=0, tiled=True),
-        lax.psum_scatter(terms[6], ("clip", "blk"), scatter_dimension=0, tiled=True),
-        lax.psum_scatter(terms[7], ("clip", "blk"), scatter_dimension=0, tiled=True),
-        lax.psum_scatter(terms[8], ("clip", "blk"), scatter_dimension=0, tiled=True),
-        lax.psum_scatter(terms[9], ("clip", "blk"), scatter_dimension=0, tiled=True),
-        lax.psum_scatter(terms[10], ("clip", "blk"), scatter_dimension=0, tiled=True),
-        lax.psum_scatter(terms[11], ("clip", "blk"), scatter_dimension=0, tiled=True),
-        lax.psum_scatter(terms[12], ("clip", "blk"), scatter_dimension=0, tiled=True),
-        lax.psum_scatter(terms[13], ("clip", "blk"), scatter_dimension=0, tiled=True),
-        lax.psum_scatter(terms[14], ("clip", "blk"), scatter_dimension=0, tiled=True),
-        lax.psum_scatter(terms[15], ("clip", "blk"), scatter_dimension=0, tiled=True),
-    )
+    matrices = [m.astype(jnp.bfloat16).reshape(devices, m.shape[0] // devices, m.shape[1]) for m in matrices]
+    kinds = [(1, 9, j) for j in range(4)] + [(0, 8, j) for j in range(4)] + [(0, j, 0) for j in range(8)]
+    vectors = [first_gain_term, first_shift_term, second_gain_term, second_shift_term, third_gain_term, third_shift_term]
+    stacked = jnp.stack(vectors + [jnp.zeros_like(first_gain_term)] * 2)
+    *summed, vec_sum = reduce_scatter(matrices, kinds, stacked, clip_total, block_total)
+    own = D // devices
+    vec_own = lax.dynamic_slice_in_dim(vec_sum, (lax.axis_index("clip") * block_total + block_rank) * own, own, 1)
+    summed = list(summed) + [vec_own[j] for j in range(6)]
     return (
         output_frames,
         frames_grad,

time: 1830 us -> 787 us (0.43)
  waiting for transfers between devices: 1250 us -> 123 us
  Pallas kernels: 0 us -> 196 us
  blocking collectives: 45.8 us -> 0 us
  starting transfers between devices: 235 us -> 190 us
  matrix products: 151 us -> 127 us
    reduce_scatter x10 -> x0, waiting for transfers between devices: 1110 us -> none  [the longest x1 187 us: body(): lax.psum_scatter(terms[9], ('clip', 'blk'), scatter_dimension=0, tiled=True)]
    pallas_call x0 -> x1, Pallas kernels: none -> 196 us  [reduce_scatter(): pl.pallas_call(partial(scatter_kernel, clips, blks, kinds), out_shape=[ja...]
    unnamed x1 -> x0, blocking collectives: 45.8 us -> none
    ppermute x16, waiting for transfers between devices: 73.1 us -> 29.9 us  [shifted(): return lax.ppermute(block, axis, route)]
    ppermute x16, starting transfers between devices: 113 us -> 87.2 us  [shifted(): return lax.ppermute(block, axis, route)]
    unnamed x16 -> x6, waiting for transfers between devices: 0.27 us -> 23.3 us
    ppermute x14, starting transfers between devices: 121 us -> 102 us  [shifted_2(): return lax.ppermute(block, axis, route)]
  transfers between devices with their start and end apart: 44 -> 34, of which waited for: 16 -> 7; matrix products, arithmetic and copies ran while one was open for 10% -> 18% of each run, Pallas kernels for 0% -> 0%
where the time goes in v1:
time: 787 us; the launch traced here: 775 us
  Pallas kernels  196 us (25%)
  starting transfers between devices  190 us (24%)
  matrix products  127 us (16%)
  waiting for transfers between devices  123 us (16%)
  local copies, waits for them, and re-layouts  65.8 us (8%)
  other arithmetic  56.8 us (7%)
  between operations  15.7 us (2%)
    pallas_call x1, Pallas kernels, reduce_scatter(): pl.pallas_call(partial(scatter_kernel, clips, blks, kinds), out_shape=[ja...  196 us
    ppermute x14, starting transfers between devices, shifted_2(): return lax.ppermute(block, axis, route)  102 us
    ppermute x16, starting transfers between devices, shifted(): return lax.ppermute(block, axis, route)  87.2 us
    dot_general x10, matrix products, project(): return jnp.dot(left, right, preferred_element_type=jnp.float32)  43 us
    all_gather x1, waiting for transfers between devices, body(): piece_keys = lax.all_gather(keys_local, 'blk', axis=0, tiled=True)  41.5 us
    dot_general x10, matrix products, weight_term(): jnp.einsum('td,te->de', left, right, preferred_element_type=jnp.float32)  32.5 us
    unnamed x150, local copies, waits for them, and re-layouts  30.9 us
    ppermute x16, waiting for transfers between devices, shifted(): return lax.ppermute(block, axis, route)  29.9 us
  transfers between devices with their start and end apart: 34, of which 7 were waited for; matrix products, arithmetic and copies ran while one was open for 18% of the time, Pallas kernels for 0%

profile of v1, /device:TPU:0, one launch (start us, length us, event | category | flops | bytes accessed | tf_op | source)
XLA Modules:
  0.0 775.2 jit_solution(10405188821286080577)
XLA Ops:
  36.1 27.8 %all-gather.5.cloned.1.call-done = bf16[2048,1024]{1,0:T(8,128)(2,1)} async-done(((bf16[256,1024]{1,0:T(8,128)(2,1)}), bf16[2048,1024]{1,0:T(8,128)(2,1)}) %all-gather.5.cloned.1.call-update) | async-done | bytes 4194320 | tf_op jit(solution)/shard_map/all_gather | solution.py:294
  70.4 41.5 %all-gather.3.cloned.1.call-done = bf16[2048,1024]{1,0:T(8,128)(2,1)} async-done(((bf16[256,1024]{1,0:T(8,128)(2,1)}), bf16[2048,1024]{1,0:T(8,128)(2,1)}) %all-gather.3.cloned.1.call-update) | async-done | bytes 4194320 | tf_op jit(solution)/shard_map/all_gather | solution.py:293
  146.2 15.5 %multiply_convert_fusion.3 = (bf16[256,4096]{1,0:T(8,128)(2,1)}, f32[256,4096]{1,0:T(8,128)S(1)}, f32[256,4096]{1,0:T(8,128)}) fusion(bf16[1024,4096]{1,0:T(8,128)(2,1)} %param.42, f32[256,1024]{1,0:T(8,128)S(1)} %get-tuple-element.865, f32[1024]{0:T(1024)S(1)} %copy-done.65, f32[1024]{0:T(1024)S(1)} %copy-done.64, f32[256]{0:T(256)S(1)} %fusion.92, ...), kind=kOutput, calls=%fused_computation.62 | convolution fusion | flops 2216951808 | bytes 19933184 | tf_op jit(solution)/shard_map/dot_general | solution.py:37
  161.7 11.1 %add_convert_fusion = bf16[256,4096]{1,0:T(8,128)(2,1)S(1)} fusion(f32[256,4096]{1,0:T(8,128)S(1)} %get-tuple-element.841, f32[256,4096]{1,0:T(8,128)} %get-tuple-element.866, bf16[4096,1024]{1,0:T(8,128)(2,1)} %param.43, bf16[1,256,1024]{2,1,0:T(8,128)(2,1)S(1)} %copy-done.22), kind=kOutput, calls=%fused_computation.61 | convolution fusion | flops 2162163712 | bytes 19398656 | tf_op jit(solution)/shard_map/te,de->td/dot_general | solution.py:45
  172.8 6.8 multiply_reduce_fusion.1
  219.5 260.1 %while.43 = (s32[]{:T(128)}, bf16[256,1024]{0,1:T(8,128)(2,1)S(1)}, bf16[256,1024]{0,1:T(8,128)(2,1)}, f32[256,1024]{0,1:T(8,128)}, f32[256,1024]{0,1:T(8,128)},...) while((s32[]{:T(128)}, bf16[256,1024]{0,1:T(8,128)(2,1)S(1)}, ...), condition=%wide.region_23.24_spmd.clone, body=%wide.region_20.0_spmd.clone.sunk | while | flops 686621184 | bytes 66837216 | solution.py:504
  240.7 7.7 collective-permute-start
  248.4 9.7 %collective-permute-start.1 = (bf16[256,1024]{0,1:T(8,128)(2,1)}, bf16[256,1024]{0,1:T(8,128)(2,1)}, u32[]{:S(2)}, u32[]{:S(2)}) collective-permute-start(bf16[256,1024]{0,1:T(8,128)(2,1)} %copy.137), channel_id=1, source_target_pairs={{0,1},{1,2},{2,3},{3,4},{4,5},{5,6},{6,7},{8,9},{9,10},{10,11},{11... | collective-permute-start | bytes 1572872 | tf_op jit(solution)/shard_map/while/body/eval_jaxpr/ppermute | solution.py:27
  258.1 17.9 %collective-permute-done.3 = bf16[256,1024]{0,1:T(8,128)(2,1)S(1)} collective-permute-done((bf16[256,1024]{0,1:T(8,128)(2,1)}, bf16[256,1024]{0,1:T(8,128)(2,1)S(1)}, u32[]{:S(2)}, u32[]{:S(2)}) %collective-permute-start.3) | collective-permute-done | bytes 524320 | tf_op jit(solution)/shard_map/while/body/eval_jaxpr/ppermute | solution.py:21
  288.1 6.9 collective-permute-start
  316.8 8.7 %collective-permute-start.2 = (bf16[256,1024]{0,1:T(8,128)(2,1)}, bf16[256,1024]{0,1:T(8,128)(2,1)S(1)}, u32[]{:S(2)}, u32[]{:S(2)}) collective-permute-start(bf16[256,1024]{0,1:T(8,128)(2,1)} %convert_element_type.438), channel_id=1, source_target_pairs={{7,0},{0,1},{1,2},{2,3},{3,4},{4,5},{5,6},{6,7},{15,8},{8,9},{9,10... | collective-permute-start | bytes 1572872 | tf_op jit(solution)/shard_map/while/body/eval_jaxpr/ppermute | solution.py:21
  325.6 6.9 collective-permute-start
  344.2 8.4 %collective-permute-start.3 = (bf16[256,1024]{0,1:T(8,128)(2,1)}, bf16[256,1024]{0,1:T(8,128)(2,1)S(1)}, u32[]{:S(2)}, u32[]{:S(2)}) collective-permute-start(bf16[256,1024]{0,1:T(8,128)(2,1)} %convert_element_type.440), channel_id=1, source_target_pairs={{7,0},{0,1},{1,2},{2,3},{3,4},{4,5},{5,6},{6,7},{15,8},{8,9},{9,10... | collective-permute-start | bytes 1572872 | tf_op jit(solution)/shard_map/while/body/eval_jaxpr/ppermute | solution.py:21
  356.0 13.0 %collective-permute-start = (bf16[256,1024]{0,1:T(8,128)(2,1)S(1)}, bf16[256,1024]{0,1:T(8,128)(2,1)S(1)}, u32[]{:S(2)}, u32[]{:S(2)}) collective-permute-start(bf16[256,1024]{0,1:T(8,128)(2,1)S(1)} %copy.136), channel_id=1, source_target_pairs={{0,1},{1,2},{2,3},{3,4},{4,5},{5,6},{6,7},{8,9},{9,10},{10,11},{11... | collective-permute-start | bytes 1572872 | tf_op jit(solution)/shard_map/while/body/eval_jaxpr/ppermute | solution.py:27
  380.8 8.4 %collective-permute-start.3 = (bf16[256,1024]{0,1:T(8,128)(2,1)}, bf16[256,1024]{0,1:T(8,128)(2,1)S(1)}, u32[]{:S(2)}, u32[]{:S(2)}) collective-permute-start(bf16[256,1024]{0,1:T(8,128)(2,1)} %convert_element_type.440), channel_id=1, source_target_pairs={{7,0},{0,1},{1,2},{2,3},{3,4},{4,5},{5,6},{6,7},{15,8},{8,9},{9,10... | collective-permute-start | bytes 1572872 | tf_op jit(solution)/shard_map/while/body/eval_jaxpr/ppermute | solution.py:21
  392.6 6.7 collective-permute-start
  399.3 11.4 %collective-permute-start.1 = (bf16[256,1024]{0,1:T(8,128)(2,1)}, bf16[256,1024]{0,1:T(8,128)(2,1)}, u32[]{:S(2)}, u32[]{:S(2)}) collective-permute-start(bf16[256,1024]{0,1:T(8,128)(2,1)} %copy.137), channel_id=1, source_target_pairs={{0,1},{1,2},{2,3},{3,4},{4,5},{5,6},{6,7},{8,9},{9,10},{10,11},{11... | collective-permute-start | bytes 1572872 | tf_op jit(solution)/shard_map/while/body/eval_jaxpr/ppermute | solution.py:27
  417.3 8.3 %collective-permute-start.3 = (bf16[256,1024]{0,1:T(8,128)(2,1)}, bf16[256,1024]{0,1:T(8,128)(2,1)S(1)}, u32[]{:S(2)}, u32[]{:S(2)}) collective-permute-start(bf16[256,1024]{0,1:T(8,128)(2,1)} %convert_element_type.440), channel_id=1, source_target_pairs={{7,0},{0,1},{1,2},{2,3},{3,4},{4,5},{5,6},{6,7},{15,8},{8,9},{9,10... | collective-permute-start | bytes 1572872 | tf_op jit(solution)/shard_map/while/body/eval_jaxpr/ppermute | solution.py:21
  428.9 6.9 collective-permute-start
  447.6 14.5 %collective-permute-start.3 = (bf16[256,1024]{0,1:T(8,128)(2,1)}, bf16[256,1024]{0,1:T(8,128)(2,1)S(1)}, u32[]{:S(2)}, u32[]{:S(2)}) collective-permute-start(bf16[256,1024]{0,1:T(8,128)(2,1)} %convert_element_type.440), channel_id=1, source_target_pairs={{7,0},{0,1},{1,2},{2,3},{3,4},{4,5},{5,6},{6,7},{15,8},{8,9},{9,10... | collective-permute-start | bytes 1572872 | tf_op jit(solution)/shard_map/while/body/eval_jaxpr/ppermute | solution.py:21
  465.4 6.9 collective-permute-start
  485.3 8.4 %collective-permute-start.5 = (bf16[256,1024]{0,1:T(8,128)(2,1)}, bf16[256,1024]{0,1:T(8,128)(2,1)}, u32[]{:S(2)}, u32[]{:S(2)}) collective-permute-start(bf16[256,1024]{0,1:T(8,128)(2,1)} %convert_element_type.275), channel_id=1, source_target_pairs={{7,0},{0,1},{1,2},{2,3},{3,4},{4,5},{5,6},{6,7},{15,8},{8,9},{9,10... | collective-permute-start | bytes 1572872 | tf_op jit(solution)/shard_map/ppermute | solution.py:21
  535.0 23.3 %reduce-scatter.7.cloned.1.call-done = bf16[32,1024]{1,0:T(8,128)(2,1)} async-done(((bf16[256,1024]{1,0:T(8,128)(2,1)}), bf16[32,1024]{1,0:T(8,128)(2,1)}) %reduce-scatter.7.cloned.1.call-update) | async-done | bytes 65552
  561.2 196.5 %shard_map.339 = (f32[32,1024]{1,0:T(8,128)}, f32[32,1024]{1,0:T(8,128)}, f32[32,1024]{1,0:T(8,128)}, f32[32,1024]{1,0:T(8,128)}, f32[32,1024]{1,0:T(8,128)}, /*...) custom-call(bf16[32,32,1024]{2,1,0:T(8,128)(2,1)} %bitcast.249, ...), custom_call_target="tpu_custom_call" | custom-call | tf_op jit(solution)/shard_map/pallas_call | solution.py:244
  (396 shorter events, 303.4 us)
Async XLA Ops:
  7.2 56.7 %all-gather.5.cloned.1.call-start = ((), (), s32[]{:S(2)}) async-start(), calls=%async_computation.3 | async-start | bytes 4718592 | tf_op jit(solution)/shard_map/all_gather | solution.py:294
  13.9 98.0 %all-gather.3.cloned.1.call-start = ((), (), s32[]{:S(2)}) async-start(), calls=%async_computation.2 | async-start | bytes 4718592 | tf_op jit(solution)/shard_map/all_gather | solution.py:293
  17.2 514.9 %reduce-scatter.9.cloned.1.call-start = ((), (), s32[]{:S(2)}) async-start(), calls=%async_computation.5 | async-start | bytes 589824
  205.9 352.4 %reduce-scatter.7.cloned.1.call-start = ((), (), s32[]{:S(2)}) async-start(), calls=%async_computation.4 | async-start | bytes 589824
  228.8 47.3 %collective-permute-start.3 = (bf16[256,1024]{0,1:T(8,128)(2,1)}, bf16[256,1024]{0,1:T(8,128)(2,1)S(1)}, u32[]{:S(2)}, u32[]{:S(2)}) collective-permute-start(bf16[256,1024]{0,1:T(8,128)(2,1)} %convert_element_type.440), channel_id=1, source_target_pairs={{7,0},{0,1},{1,2},{2,3},{3,4},{4,5},{5,6},{6,7},{15,8},{8,9},{9,10... | collective-permute-start | bytes 1572872 | tf_op jit(solution)/shard_map/while/body/eval_jaxpr/ppermute | solution.py:21
  235.4 46.3 %collective-permute-start.2 = (bf16[256,1024]{0,1:T(8,128)(2,1)}, bf16[256,1024]{0,1:T(8,128)(2,1)S(1)}, u32[]{:S(2)}, u32[]{:S(2)}) collective-permute-start(bf16[256,1024]{0,1:T(8,128)(2,1)} %convert_element_type.438), channel_id=1, source_target_pairs={{7,0},{0,1},{1,2},{2,3},{3,4},{4,5},{5,6},{6,7},{15,8},{8,9},{9,10... | collective-permute-start | bytes 1572872 | tf_op jit(solution)/shard_map/while/body/eval_jaxpr/ppermute | solution.py:21
  240.7 42.0 %collective-permute-start = (bf16[256,1024]{0,1:T(8,128)(2,1)S(1)}, bf16[256,1024]{0,1:T(8,128)(2,1)S(1)}, u32[]{:S(2)}, u32[]{:S(2)}) collective-permute-start(bf16[256,1024]{0,1:T(8,128)(2,1)S(1)} %copy.136), channel_id=1, source_target_pairs={{0,1},{1,2},{2,3},{3,4},{4,5},{5,6},{6,7},{8,9},{9,10},{10,11},{11... | collective-permute-start | bytes 1572872 | tf_op jit(solution)/shard_map/while/body/eval_jaxpr/ppermute | solution.py:27
  248.4 34.3 %collective-permute-start.1 = (bf16[256,1024]{0,1:T(8,128)(2,1)}, bf16[256,1024]{0,1:T(8,128)(2,1)}, u32[]{:S(2)}, u32[]{:S(2)}) collective-permute-start(bf16[256,1024]{0,1:T(8,128)(2,1)} %copy.137), channel_id=1, source_target_pairs={{0,1},{1,2},{2,3},{3,4},{4,5},{5,6},{6,7},{8,9},{9,10},{10,11},{11... | collective-permute-start | bytes 1572872 | tf_op jit(solution)/shard_map/while/body/eval_jaxpr/ppermute | solution.py:27
  288.0 17.5 %collective-permute-start.2 = (bf16[256,1024]{0,1:T(8,128)(2,1)}, bf16[256,1024]{0,1:T(8,128)(2,1)S(1)}, u32[]{:S(2)}, u32[]{:S(2)}) collective-permute-start(bf16[256,1024]{0,1:T(8,128)(2,1)} %convert_element_type.438), channel_id=1, source_target_pairs={{7,0},{0,1},{1,2},{2,3},{3,4},{4,5},{5,6},{6,7},{15,8},{8,9},{9,10... | collective-permute-start | bytes 1572872 | tf_op jit(solution)/shard_map/while/body/eval_jaxpr/ppermute | solution.py:21
  288.1 18.5 %collective-permute-start = (bf16[256,1024]{0,1:T(8,128)(2,1)S(1)}, bf16[256,1024]{0,1:T(8,128)(2,1)S(1)}, u32[]{:S(2)}, u32[]{:S(2)}) collective-permute-start(bf16[256,1024]{0,1:T(8,128)(2,1)S(1)} %copy.136), channel_id=1, source_target_pairs={{0,1},{1,2},{2,3},{3,4},{4,5},{5,6},{6,7},{8,9},{9,10},{10,11},{11... | collective-permute-start | bytes 1572872 | tf_op jit(solution)/shard_map/while/body/eval_jaxpr/ppermute | solution.py:27
  311.1 26.5 %collective-permute-start.3 = (bf16[256,1024]{0,1:T(8,128)(2,1)}, bf16[256,1024]{0,1:T(8,128)(2,1)S(1)}, u32[]{:S(2)}, u32[]{:S(2)}) collective-permute-start(bf16[256,1024]{0,1:T(8,128)(2,1)} %convert_element_type.440), channel_id=1, source_target_pairs={{7,0},{0,1},{1,2},{2,3},{3,4},{4,5},{5,6},{6,7},{15,8},{8,9},{9,10... | collective-permute-start | bytes 1572872 | tf_op jit(solution)/shard_map/while/body/eval_jaxpr/ppermute | solution.py:21
  316.8 21.9 %collective-permute-start.2 = (bf16[256,1024]{0,1:T(8,128)(2,1)}, bf16[256,1024]{0,1:T(8,128)(2,1)S(1)}, u32[]{:S(2)}, u32[]{:S(2)}) collective-permute-start(bf16[256,1024]{0,1:T(8,128)(2,1)} %convert_element_type.438), channel_id=1, source_target_pairs={{7,0},{0,1},{1,2},{2,3},{3,4},{4,5},{5,6},{6,7},{15,8},{8,9},{9,10... | collective-permute-start | bytes 1572872 | tf_op jit(solution)/shard_map/while/body/eval_jaxpr/ppermute | solution.py:21
  344.2 29.9 %collective-permute-start.3 = (bf16[256,1024]{0,1:T(8,128)(2,1)}, bf16[256,1024]{0,1:T(8,128)(2,1)S(1)}, u32[]{:S(2)}, u32[]{:S(2)}) collective-permute-start(bf16[256,1024]{0,1:T(8,128)(2,1)} %convert_element_type.440), channel_id=1, source_target_pairs={{7,0},{0,1},{1,2},{2,3},{3,4},{4,5},{5,6},{6,7},{15,8},{8,9},{9,10... | collective-permute-start | bytes 1572872 | tf_op jit(solution)/shard_map/while/body/eval_jaxpr/ppermute | solution.py:21
  353.5 21.7 %collective-permute-start.2 = (bf16[256,1024]{0,1:T(8,128)(2,1)}, bf16[256,1024]{0,1:T(8,128)(2,1)S(1)}, u32[]{:S(2)}, u32[]{:S(2)}) collective-permute-start(bf16[256,1024]{0,1:T(8,128)(2,1)} %convert_element_type.438), channel_id=1, source_target_pairs={{7,0},{0,1},{1,2},{2,3},{3,4},{4,5},{5,6},{6,7},{15,8},{8,9},{9,10... | collective-permute-start | bytes 1572872 | tf_op jit(solution)/shard_map/while/body/eval_jaxpr/ppermute | solution.py:21
  356.0 20.3 %collective-permute-start = (bf16[256,1024]{0,1:T(8,128)(2,1)S(1)}, bf16[256,1024]{0,1:T(8,128)(2,1)S(1)}, u32[]{:S(2)}, u32[]{:S(2)}) collective-permute-start(bf16[256,1024]{0,1:T(8,128)(2,1)S(1)} %copy.136), channel_id=1, source_target_pairs={{0,1},{1,2},{2,3},{3,4},{4,5},{5,6},{6,7},{8,9},{9,10},{10,11},{11... | collective-permute-start | bytes 1572872 | tf_op jit(solution)/shard_map/while/body/eval_jaxpr/ppermute | solution.py:27
  380.8 29.9 %collective-permute-start.3 = (bf16[256,1024]{0,1:T(8,128)(2,1)}, bf16[256,1024]{0,1:T(8,128)(2,1)S(1)}, u32[]{:S(2)}, u32[]{:S(2)}) collective-permute-start(bf16[256,1024]{0,1:T(8,128)(2,1)} %convert_element_type.440), channel_id=1, source_target_pairs={{7,0},{0,1},{1,2},{2,3},{3,4},{4,5},{5,6},{6,7},{15,8},{8,9},{9,10... | collective-permute-start | bytes 1572872 | tf_op jit(solution)/shard_map/while/body/eval_jaxpr/ppermute | solution.py:21
  390.1 21.7 %collective-permute-start.2 = (bf16[256,1024]{0,1:T(8,128)(2,1)}, bf16[256,1024]{0,1:T(8,128)(2,1)S(1)}, u32[]{:S(2)}, u32[]{:S(2)}) collective-permute-start(bf16[256,1024]{0,1:T(8,128)(2,1)} %convert_element_type.438), channel_id=1, source_target_pairs={{7,0},{0,1},{1,2},{2,3},{3,4},{4,5},{5,6},{6,7},{15,8},{8,9},{9,10... | collective-permute-start | bytes 1572872 | tf_op jit(solution)/shard_map/while/body/eval_jaxpr/ppermute | solution.py:21
  392.6 20.3 %collective-permute-start = (bf16[256,1024]{0,1:T(8,128)(2,1)S(1)}, bf16[256,1024]{0,1:T(8,128)(2,1)S(1)}, u32[]{:S(2)}, u32[]{:S(2)}) collective-permute-start(bf16[256,1024]{0,1:T(8,128)(2,1)S(1)} %copy.136), channel_id=1, source_target_pairs={{0,1},{1,2},{2,3},{3,4},{4,5},{5,6},{6,7},{8,9},{9,10},{10,11},{11... | collective-permute-start | bytes 1572872 | tf_op jit(solution)/shard_map/while/body/eval_jaxpr/ppermute | solution.py:27
  417.3 23.7 %collective-permute-start.3 = (bf16[256,1024]{0,1:T(8,128)(2,1)}, bf16[256,1024]{0,1:T(8,128)(2,1)S(1)}, u32[]{:S(2)}, u32[]{:S(2)}) collective-permute-start(bf16[256,1024]{0,1:T(8,128)(2,1)} %convert_element_type.440), channel_id=1, source_target_pairs={{7,0},{0,1},{1,2},{2,3},{3,4},{4,5},{5,6},{6,7},{15,8},{8,9},{9,10... | collective-permute-start | bytes 1572872 | tf_op jit(solution)/shard_map/while/body/eval_jaxpr/ppermute | solution.py:21
  426.4 15.6 %collective-permute-start.2 = (bf16[256,1024]{0,1:T(8,128)(2,1)}, bf16[256,1024]{0,1:T(8,128)(2,1)S(1)}, u32[]{:S(2)}, u32[]{:S(2)}) collective-permute-start(bf16[256,1024]{0,1:T(8,128)(2,1)} %convert_element_type.438), channel_id=1, source_target_pairs={{7,0},{0,1},{1,2},{2,3},{3,4},{4,5},{5,6},{6,7},{15,8},{8,9},{9,10... | collective-permute-start | bytes 1572872 | tf_op jit(solution)/shard_map/while/body/eval_jaxpr/ppermute | solution.py:21
  447.6 29.9 %collective-permute-start.3 = (bf16[256,1024]{0,1:T(8,128)(2,1)}, bf16[256,1024]{0,1:T(8,128)(2,1)S(1)}, u32[]{:S(2)}, u32[]{:S(2)}) collective-permute-start(bf16[256,1024]{0,1:T(8,128)(2,1)} %convert_element_type.440), channel_id=1, source_target_pairs={{7,0},{0,1},{1,2},{2,3},{3,4},{4,5},{5,6},{6,7},{15,8},{8,9},{9,10... | collective-permute-start | bytes 1572872 | tf_op jit(solution)/shard_map/while/body/eval_jaxpr/ppermute | solution.py:21
  463.0 15.6 %collective-permute-start.2 = (bf16[256,1024]{0,1:T(8,128)(2,1)}, bf16[256,1024]{0,1:T(8,128)(2,1)S(1)}, u32[]{:S(2)}, u32[]{:S(2)}) collective-permute-start(bf16[256,1024]{0,1:T(8,128)(2,1)} %convert_element_type.438), channel_id=1, source_target_pairs={{7,0},{0,1},{1,2},{2,3},{3,4},{4,5},{5,6},{6,7},{15,8},{8,9},{9,10... | collective-permute-start | bytes 1572872 | tf_op jit(solution)/shard_map/while/body/eval_jaxpr/ppermute | solution.py:21
  485.3 35.5 %collective-permute-start.5 = (bf16[256,1024]{0,1:T(8,128)(2,1)}, bf16[256,1024]{0,1:T(8,128)(2,1)}, u32[]{:S(2)}, u32[]{:S(2)}) collective-permute-start(bf16[256,1024]{0,1:T(8,128)(2,1)} %convert_element_type.275), channel_id=1, source_target_pairs={{7,0},{0,1},{1,2},{2,3},{3,4},{4,5},{5,6},{6,7},{15,8},{8,9},{9,10... | collective-permute-start | bytes 1572872 | tf_op jit(solution)/shard_map/ppermute | solution.py:21
  493.7 25.3 %collective-permute-start.4 = (bf16[256,1024]{0,1:T(8,128)(2,1)}, bf16[256,1024]{0,1:T(8,128)(2,1)}, u32[]{:S(2)}, u32[]{:S(2)}) collective-permute-start(bf16[256,1024]{0,1:T(8,128)(2,1)} %convert_element_type.274), channel_id=1, source_target_pairs={{7,0},{0,1},{1,2},{2,3},{3,4},{4,5},{5,6},{6,7},{15,8},{8,9},{9,10... | collective-permute-start | bytes 1572872 | tf_op jit(solution)/shard_map/ppermute | solution.py:21
  (83 other events, 1428.7 us)
Sparse Core Ops, SparseCore 0:
  14.0 49.8 all-gather.4
  66.1 45.7 all-gather.2
  206.0 68.7 reduce-scatter.8
  511.5 46.6 reduce-scatter.6

commit v2 on v1

--- a/solution.py
+++ b/solution.py
@@ -13,36 +13,6 @@
 HEAD = 64
 TEXT = 256
 MESH = pl.DeviceIdType.MESH
-
-
-def shifted(block, axis, distance):
-    devices = range(lax.axis_size(axis))
-    route = [((i - distance) % len(devices), i) for i in devices]
-    return lax.ppermute(block, axis, route)
-
-
-def shifted_2(block, axis, distance):
-    devices = range(lax.axis_size(axis))
-    route = [(i - distance, i) for i in devices if i - distance in devices]
-    return lax.ppermute(block, axis, route)
-
-
-def layer_norm(inputs, gain_vec, shift_vec):
-    centred = inputs - jnp.mean(inputs, axis=-1, keepdims=True)
-    variance = jnp.mean(centred * centred, axis=-1, keepdims=True)
-    return centred * lax.rsqrt(variance + 1e-05) * gain_vec + shift_vec
-
-
-def project(left, right):
-    return jnp.dot(left, right, preferred_element_type=jnp.float32)
-
-
-def weight_term(left, right):
-    return jnp.einsum("td,te->de", left, right, preferred_element_type=jnp.float32)
-
-
-def back_project(left, right):
-    return jnp.einsum("te,de->td", left, right, preferred_element_type=jnp.float32)
 
 
 def bits_of(size):
@@ -125,22 +95,27 @@
     orders = stage_orders(clips, blks)
     stages = len(orders[0])
     count = len(kinds)
+    head_w, refs = refs[0], refs[1:]
     n_kind = max(k for k, _, _ in kinds) + 1
     arrays = refs[: len(set((k, a) for k, a, _ in kinds))]
     refs = refs[len(arrays) :]
     vec, refs = refs[0], refs[1:]
     outs, refs = refs[: len(arrays)], refs[len(arrays) :]
-    vec_out, refs = refs[0], refs[1:]
+    (vec_out, head_out), refs = refs[:2], refs[2:]
+    clip_stages = bits_of(clips)
+    head_own, refs = refs[0], refs[1:]
+    head_recvs, refs = refs[:clip_stages], refs[clip_stages:]
+    (head_send, head_recv, head_sem, swap_send, swap_recv), refs = refs[:5], refs[5:]
     owns, refs = refs[:n_kind], refs[n_kind:]
     recvs, refs = refs[: n_kind * stages], refs[n_kind * stages :]
     vec_in, send_sems, recv_sems, own_sems, vec_send, vec_recv = refs
 
-    barrier = pltpu.get_barrier_semaphore()
     for axis, bit in orders[0]:
-        me = lax.axis_index(axis)
-        partner = me + (1 << bit) * (1 - 2 * ((me // (1 << bit)) % 2))
-        pl.semaphore_signal(barrier, inc=1, device_id={axis: partner}, device_id_type=MESH)
-    pl.semaphore_wait(barrier, stages)
+        if axis == "clip":
+            me = lax.axis_index(axis)
+            partner = me + (1 << bit) * (1 - 2 * ((me // (1 << bit)) % 2))
+            pl.semaphore_signal(pltpu.get_barrier_semaphore(), inc=1, device_id={axis: partner}, device_id_type=MESH)
+    greet("blk", clip_stages)
 
     pieces, targets = [], []
     seen = [0] * n_kind
@@ -174,8 +149,23 @@
             device_id_type=MESH,
         )
 
+    everything = slice(None)
+    heads = Scatter(
+        [("clip", k) for k in range(clip_stages)], clips, blks, head_w, everything, head_own, list(head_recvs),
+        head_send, head_recv, head_sem,
+    )
+    rank = lax.axis_index("blk")
+
+    def swap(peer, source):
+        return pltpu.make_async_remote_copy(
+            src_ref=head_recvs[-1].at[peer], dst_ref=head_out.at[source], send_sem=swap_send.at[peer],
+            recv_sem=swap_recv.at[source], device_id={"blk": peer}, device_id_type=MESH,
+        )
+
     vec_in[0, 0] = vec[...]
     vec_copy(0).start()
+    heads.copy(0).start()
+    heads.load().start()
     for piece in pieces:
         piece.copy(0).start()
     held = {}
@@ -208,6 +198,17 @@
                 kind = kinds[p][0]
                 done[kind] += 1
                 load_ahead(kind, slots[kind] + done[kind])
+        if stage < clip_stages:
+            heads.copy(stage).wait()
+            if stage == 0:
+                heads.load().wait()
+            heads.add(stage)
+            if stage + 1 < clip_stages:
+                heads.copy(stage + 1).start()
+            else:
+                head_out[rank] = head_recvs[-1][rank]
+                for step in range(1, blks):
+                    swap((rank + step) % blks, rank).start()
         vec_copy(stage).wait()
         summed = vec_in[0, stage] + vec_in[1, stage]
         if stage == stages - 1:
@@ -215,9 +216,13 @@
         else:
             vec_in[0, stage + 1] = summed
             vec_copy(stage + 1).start()
-
-
-def reduce_scatter(arrays, kinds, vec, clips, blks):
+    for step in range(1, blks):
+        peer = (rank + step) % blks
+        swap(peer, rank).wait_send()
+        swap(peer, peer).wait_recv()
+
+
+def reduce_scatter(head_w, arrays, kinds, vec, clips, blks):
     orders = stage_orders(clips, blks)
     stages = len(orders[0])
     devices = clips * blks
@@ -232,23 +237,383 @@
         shapes[kind] = (arrays[array].shape[1], arrays[array].shape[2] // parts_of[array])
     any_spec = pl.BlockSpec(memory_space=pltpu.MemorySpace.HBM)
     vmem = pl.BlockSpec(memory_space=pltpu.VMEM)
-    scratch = [pltpu.VMEM((min(3, totals[k]), devices // 2, *shapes[k]), jnp.bfloat16) for k in range(n_kind)]
+    clip_stages = bits_of(clips)
+    dma = pltpu.SemaphoreType.DMA
+    head_shape = head_w.shape[1:]
+    scratch = [pltpu.VMEM((devices // 2, *head_shape), jnp.bfloat16)]
+    scratch += [pltpu.VMEM((devices >> (s + 1), *head_shape), jnp.bfloat16) for s in range(clip_stages)]
+    scratch += [dma((clip_stages,)), dma((clip_stages,)), dma, dma((blks,)), dma((blks,))]
+    scratch += [pltpu.VMEM((min(3, totals[k]), devices // 2, *shapes[k]), jnp.bfloat16) for k in range(n_kind)]
     for k in range(n_kind):
         for s in range(stages):
             scratch.append(pltpu.VMEM((totals[k], devices >> (s + 1), *shapes[k]), jnp.bfloat16))
-    dma = pltpu.SemaphoreType.DMA
     scratch += [
         pltpu.VMEM((2, stages, *vec.shape), jnp.float32),
         dma((count, stages)), dma((count, stages)), dma((count,)), dma((stages,)), dma((stages,)),
     ]
     return pl.pallas_call(
         partial(scatter_kernel, clips, blks, kinds),
-        out_shape=[jax.ShapeDtypeStruct(a.shape[1:], jnp.float32) for a in arrays] + [jax.ShapeDtypeStruct(vec.shape, jnp.float32)],
-        in_specs=[any_spec] * len(arrays) + [vmem],
-        out_specs=[vmem] * (len(arrays) + 1),
+        out_shape=[jax.ShapeDtypeStruct(a.shape[1:], jnp.float32) for a in arrays]
+        + [jax.ShapeDtypeStruct(vec.shape, jnp.float32), jax.ShapeDtypeStruct((blks, *head_shape), jnp.bfloat16)],
+        in_specs=[any_spec] * (1 + len(arrays)) + [vmem],
+        out_specs=[vmem] * (len(arrays) + 2),
         scratch_shapes=scratch,
         compiler_params=pltpu.CompilerParams(collective_id=0, has_side_effects=True, vmem_limit_bytes=56 << 20),
-    )(*arrays, vec)
+    )(head_w, *arrays, vec)
+
+
+def normed(block, gain, shift):
+    values = block.astype(jnp.float32)
+    centred = values - jnp.mean(values, axis=-1, keepdims=True)
+    variance = jnp.mean(centred * centred, axis=-1, keepdims=True)
+    return centred * lax.rsqrt(variance + 1e-05) * gain + shift
+
+
+def matmul(left, right, over=(1, 0)):
+    return lax.dot_general(left, right, (((over[0],), (over[1],)), ((), ())), preferred_element_type=jnp.float32)
+
+
+def greet(axis, others):
+    me, size = lax.axis_index(axis), lax.axis_size(axis)
+    barrier = pltpu.get_barrier_semaphore()
+    for step in range(1, size):
+        pl.semaphore_signal(barrier, inc=1, device_id={axis: (me + step) % size}, device_id_type=MESH)
+    pl.semaphore_wait(barrier, size - 1 + others)
+
+
+def head_only(block, head):
+    lanes = block.shape[-1]
+    if lanes == HEAD:
+        return block
+    lane = lax.broadcasted_iota(jnp.int32, block.shape, 1)
+    return jnp.where((lane // HEAD) == head, block, jnp.zeros_like(block))
+
+
+def causal(rows, transposed):
+    row = lax.broadcasted_iota(jnp.int32, (rows, rows), 0)
+    column = lax.broadcasted_iota(jnp.int32, (rows, rows), 1)
+    return (row <= column) if transposed else (column <= row)
+
+
+def forward_kernel(
+    frames, weight, gain, shift, att_out, act_out, qkv_out, full_out, lse_out, gathered, low, ring_send, ring_recv, core_send, core_recv, out_send, out_recv
+):
+    blks = lax.axis_size("blk")
+    chips = blks // 2
+    me = lax.axis_index("blk")
+    chip, core = me // 2, me % 2
+    rows, width = low.shape[1:]
+    heads = width // HEAD
+
+    greet("blk", 0)
+    gathered[me] = frames[...]
+
+    def ring(slot, way):
+        return pltpu.make_async_remote_copy(
+            src_ref=gathered.at[slot], dst_ref=gathered.at[slot], send_sem=ring_send.at[0 if way > 0 else 1, slot],
+            recv_sem=ring_recv.at[slot], device_id={"blk": me + 2 * way}, device_id_type=MESH,
+        )
+
+    def across(slot):
+        return pltpu.make_async_remote_copy(
+            src_ref=gathered.at[slot], dst_ref=gathered.at[slot], send_sem=core_send.at[slot],
+            recv_sem=core_recv.at[slot], device_id={"blk": chip * 2 + 1 - core}, device_id_type=MESH,
+        )
+
+    def project_block(slot):
+        act = normed(gathered[slot], gain[...], shift[...]).astype(jnp.bfloat16)
+        act_out[slot] = act
+        made = matmul(act, weight[...]).astype(jnp.bfloat16)
+        qkv_out[slot, :, :width] = made[:, :width] * jnp.bfloat16(0.125)
+        qkv_out[slot, :, width:] = made[:, width:]
+
+    @pl.when(chip + 1 < chips)
+    def _():
+        ring(me, 1).start()
+
+    @pl.when(chip > 0)
+    def _():
+        ring(me, -1).start()
+
+    across(me).start()
+    project_block(me)
+    other = chip * 2 + 1 - core
+    across(other).wait_recv()
+    project_block(other)
+
+    for step in range(1, chips):
+        for way in (1, -1):
+            source = chip - way * step
+
+            @pl.when((source >= 0) & (source < chips))
+            def _():
+                slot = source * 2 + core
+                ring(slot, way).wait_recv()
+
+                @pl.when((chip + way >= 0) & (chip + way < chips))
+                def _():
+                    ring(slot, way).start()
+
+                across(slot).start()
+
+        for way in (1, -1):
+            source = chip - way * step
+
+            @pl.when((source >= 0) & (source < chips))
+            def _():
+                project_block(source * 2 + core)
+                across(source * 2 + 1 - core).wait_recv()
+                project_block(source * 2 + 1 - core)
+
+    mask = causal(rows, False)
+
+    def send(block):
+        return pltpu.make_async_remote_copy(
+            src_ref=low.at[block], dst_ref=att_out.at[me], send_sem=out_send.at[block],
+            recv_sem=out_recv.at[me], device_id={"blk": block}, device_id_type=MESH,
+        )
+
+    def query_block(i, carry):
+        queries = qkv_out[i, :, :width]
+        split = [head_only(queries, h) for h in range(heads)]
+
+        def update(j, state, masked):
+            keys = qkv_out[j, :, width : 2 * width]
+            values = qkv_out[j, :, 2 * width :]
+            new = []
+            for h in range(heads):
+                peak, total, acc = state[3 * h : 3 * h + 3]
+                scores = matmul(split[h], keys, (1, 1))
+                if masked:
+                    scores = jnp.where(mask, scores, -1e30)
+                top = jnp.maximum(peak, jnp.max(scores, axis=-1, keepdims=True))
+                weights = jnp.exp(scores - top)
+                rescale = jnp.exp(peak - top)
+                total = total * rescale + jnp.sum(weights, axis=-1, keepdims=True)
+                acc = acc * rescale + matmul(weights.astype(jnp.bfloat16), values)
+                new += [top, total, acc]
+            return tuple(new)
+
+        start = []
+        for _ in range(heads):
+            start += [jnp.full((rows, 1), -1e30, jnp.float32), jnp.zeros((rows, 1), jnp.float32), jnp.zeros((rows, width), jnp.float32)]
+        state = update(i, tuple(start), True)
+        state = lax.fori_loop(0, i, lambda j, held: update(j, held, False), state)
+        lane = lax.broadcasted_iota(jnp.int32, (rows, width), 1) // HEAD
+        full = state[2] / state[1]
+        stat = jnp.broadcast_to(state[0] + jnp.log(state[1]), (rows, width))
+        for h in range(1, heads):
+            full = jnp.where(lane == h, state[3 * h + 2] / state[3 * h + 1], full)
+            stat = jnp.where(lane == h, state[3 * h] + jnp.log(state[3 * h + 1]), stat)
+        full_out[i] = full
+        lse_out[i] = stat
+        low[i] = full.astype(jnp.bfloat16)
+
+        @pl.when(i != me)
+        def _():
+            send(i).start()
+
+        return carry
+
+    lax.fori_loop(0, blks, query_block, 0)
+    att_out[me] = low[me]
+
+    def finish(i, carry):
+        @pl.when(i != me)
+        def _():
+            send(i).wait_send()
+            pltpu.make_async_remote_copy(
+                src_ref=low.at[i], dst_ref=att_out.at[i], send_sem=out_send.at[i],
+                recv_sem=out_recv.at[i], device_id={"blk": i}, device_id_type=MESH,
+            ).wait_recv()
+
+        return carry
+
+    lax.fori_loop(0, blks, finish, 0)
+
+    @pl.when(chip + 1 < chips)
+    def _():
+        ring(me, 1).wait_send()
+
+    @pl.when(chip > 0)
+    def _():
+        ring(me, -1).wait_send()
+
+    across(me).wait_send()
+    for step in range(1, chips):
+        for way in (1, -1):
+            source = chip - way * step
+
+            @pl.when((source >= 0) & (source < chips))
+            def _():
+                slot = source * 2 + core
+
+                @pl.when((chip + way >= 0) & (chip + way < chips))
+                def _():
+                    ring(slot, way).wait_send()
+
+                across(slot).wait_send()
+
+
+def attention_forward(frames, weight, gain, shift, blks):
+    rows, depth = frames.shape
+    width = weight.shape[1] // 3
+    vmem = pl.BlockSpec(memory_space=pltpu.VMEM)
+    dma = pltpu.SemaphoreType.DMA
+    return pl.pallas_call(
+        forward_kernel,
+        out_shape=[
+            jax.ShapeDtypeStruct((blks, rows, width), jnp.bfloat16),
+            jax.ShapeDtypeStruct((blks, rows, depth), jnp.bfloat16),
+            jax.ShapeDtypeStruct((blks, rows, 3 * width), jnp.bfloat16),
+            jax.ShapeDtypeStruct((blks, rows, width), jnp.float32),
+            jax.ShapeDtypeStruct((blks, rows, width), jnp.float32),
+        ],
+        in_specs=[vmem] * 4,
+        out_specs=[vmem] * 5,
+        scratch_shapes=[
+            pltpu.VMEM((blks, rows, depth), jnp.bfloat16), pltpu.VMEM((blks, rows, width), jnp.bfloat16),
+            dma((2, blks)), dma((blks,)), dma((blks,)), dma((blks,)), dma((blks,)), dma((blks,)),
+        ],
+        compiler_params=pltpu.CompilerParams(collective_id=1, has_side_effects=True, vmem_limit_bytes=48 << 20),
+    )(frames, weight, gain, shift)
+
+
+def backward_kernel(
+    grads, qkv, full, lse, act, mine_out, weight_low, weight_out, grad_all, lse_rows, delta_rows, sums, query_sum, in_send, in_recv, out_send, out_recv
+):
+    blks = lax.axis_size("blk")
+    me = lax.axis_index("blk")
+    rows, width = full.shape[1:]
+    heads = width // HEAD
+    greet("blk", 0)
+
+    def fetch(peer, source):
+        return pltpu.make_async_remote_copy(
+            src_ref=grads.at[peer], dst_ref=grad_all.at[source], send_sem=in_send.at[peer],
+            recv_sem=in_recv.at[source], device_id={"blk": peer}, device_id_type=MESH,
+        )
+
+    def give(block, source):
+        return pltpu.make_async_remote_copy(
+            src_ref=sums.at[block], dst_ref=mine_out.at[source], send_sem=out_send.at[block],
+            recv_sem=out_recv.at[source], device_id={"blk": block}, device_id_type=MESH,
+        )
+
+    for step in range(1, blks):
+        fetch((me + step) % blks, me).start()
+    grad_all[me] = grads[me]
+    for i in range(blks):
+        stat = lse[i].T
+        for h in range(heads):
+            lse_rows[i, h : h + 1, :] = stat[h * HEAD : h * HEAD + 1, :]
+        query_sum[i] = jnp.zeros_like(query_sum[i])
+    for step in range(1, blks):
+        fetch((me + step) % blks, (me + step) % blks).wait_recv()
+    for i in range(blks):
+        product = (grad_all[i].astype(jnp.float32) * full[i]).T
+        for h in range(heads):
+            delta_rows[i, h : h + 1, :] = jnp.sum(product[h * HEAD : (h + 1) * HEAD], axis=0, keepdims=True)
+
+    mask = causal(rows, True)
+
+    def key_block(j, carry):
+        keys = qkv[j, :, width : 2 * width]
+        values = qkv[j, :, 2 * width :]
+        key_split = [head_only(keys, h) for h in range(heads)]
+
+        def update(i, state, masked):
+            key_sum, value_sum = state
+            queries = qkv[i, :, :width]
+            grad = grad_all[i]
+            total = None
+            for h in range(heads):
+                query_h, grad_h = head_only(queries, h), head_only(grad, h)
+                scores = matmul(keys, query_h, (1, 1))
+                probs = jnp.exp(scores - lse_rows[i, h : h + 1, :])
+                if masked:
+                    probs = jnp.where(mask, probs, 0.0)
+                dprobs = matmul(values, grad_h, (1, 1))
+                dscores = (probs * (dprobs - delta_rows[i, h : h + 1, :])).astype(jnp.bfloat16)
+                value_sum = value_sum + matmul(probs.astype(jnp.bfloat16), grad_h)
+                key_sum = key_sum + matmul(dscores, query_h)
+                term = matmul(dscores, key_split[h], (0, 0))
+                total = term if total is None else total + term
+            query_sum[i] = query_sum[i] + total
+            return key_sum, value_sum
+
+        zero = jnp.zeros((rows, width), jnp.float32)
+        state = update(j, (zero, zero), True)
+        key_sum, value_sum = lax.fori_loop(j + 1, blks, lambda i, held: update(i, held, False), state)
+        sums[j, :, :width] = (query_sum[j] * 0.125).astype(jnp.bfloat16)
+        sums[j, :, width : 2 * width] = key_sum.astype(jnp.bfloat16)
+        sums[j, :, 2 * width :] = value_sum.astype(jnp.bfloat16)
+
+        @pl.when(j != me)
+        def _():
+            give(j, me).start()
+
+        return carry
+
+    lax.fori_loop(0, blks, key_block, 0)
+    mine_out[me] = sums[me]
+    depth = act.shape[-1]
+
+    def weight_block(j, carry):
+        weight_out[...] += matmul(act[j], sums[j], (0, 0))
+        return carry
+
+    weight_out[...] = jnp.zeros_like(weight_out)
+    lax.fori_loop(0, blks, weight_block, 0)
+    weight_low[...] = weight_out[...].astype(jnp.bfloat16)
+    for step in range(1, blks):
+        peer = (me + step) % blks
+        fetch(peer, me).wait_send()
+        give(peer, me).wait_send()
+        give(peer, peer).wait_recv()
+
+
+def attention_backward(grads, qkv, full, lse, act):
+    blks, rows, width = grads.shape
+    depth = act.shape[-1]
+    vmem = pl.BlockSpec(memory_space=pltpu.VMEM)
+    dma = pltpu.SemaphoreType.DMA
+    heads = width // HEAD
+    return pl.pallas_call(
+        backward_kernel,
+        out_shape=[
+            jax.ShapeDtypeStruct((blks, rows, 3 * width), jnp.bfloat16),
+            jax.ShapeDtypeStruct((depth, 3 * width), jnp.bfloat16),
+        ],
+        in_specs=[vmem] * 5,
+        out_specs=[vmem] * 2,
+        scratch_shapes=[
+            pltpu.VMEM((depth, 3 * width), jnp.float32),
+            pltpu.VMEM((blks, rows, width), jnp.bfloat16),
+            pltpu.VMEM((blks, max(8, heads), rows), jnp.float32), pltpu.VMEM((blks, max(8, heads), rows), jnp.float32),
+            pltpu.VMEM((blks, rows, 3 * width), jnp.bfloat16), pltpu.VMEM((blks, rows, width), jnp.float32),
+            dma((blks,)), dma((blks,)), dma((blks,)), dma((blks,)),
+        ],
+        compiler_params=pltpu.CompilerParams(collective_id=2, has_side_effects=True, vmem_limit_bytes=48 << 20),
+    )(grads, qkv, full, lse, act)
+
+
+def layer_norm(inputs, gain_vec, shift_vec):
+    centred = inputs - jnp.mean(inputs, axis=-1, keepdims=True)
+    variance = jnp.mean(centred * centred, axis=-1, keepdims=True)
+    return centred * lax.rsqrt(variance + 1e-05) * gain_vec + shift_vec
+
+
+def project(left, right):
+    return jnp.dot(left, right, preferred_element_type=jnp.float32)
+
+
+def weight_term(left, right):
+    return jnp.einsum("td,te->de", left, right, preferred_element_type=jnp.float32)
+
+
+def back_project(left, right):
+    return jnp.einsum("te,de->td", left, right, preferred_element_type=jnp.float32)
 
 
 def body(
@@ -277,63 +642,21 @@
     block_rank = lax.axis_index("blk")
     local_frames = frames[0].astype(jnp.float32)
     row_count = local_frames.shape[0]
-    normed_one, norm_back_one = jax.vjp(layer_norm, local_frames, first_gain, first_shift)
-    act_one = normed_one.astype(jnp.bfloat16)
-    queries = project(act_one, self_query).astype(jnp.bfloat16)
-    keys_local = project(act_one, self_key).astype(jnp.bfloat16)
-    values_local = project(act_one, self_value).astype(jnp.bfloat16)
-    query_heads = queries.reshape(row_count, HEADS, HEAD)
-    query_index = block_rank * row_count + jnp.arange(row_count, dtype=jnp.int32)
-    query_limit = (block_rank + 1) * row_count
-    start_state = (
-        jnp.full((HEADS, row_count), -1e30, jnp.float32),
-        jnp.zeros((HEADS, row_count), jnp.float32),
-        jnp.zeros((HEADS, row_count, HEAD), jnp.float32),
-    )
-    piece_keys = lax.all_gather(keys_local, "blk", axis=0, tiled=True)
-    piece_values = lax.all_gather(values_local, "blk", axis=0, tiled=True)
-    step_rows = math.gcd(row_count, piece_keys.shape[0])
-
-    def one_step(step_index, running):
-        first_key = step_index * step_rows
-
-        def attend(running_in):
-            run_peak, run_total, weighted = running_in
-            key_block = lax.dynamic_slice_in_dim(piece_keys, step_index * step_rows, step_rows, 0)
-            value_block = lax.dynamic_slice_in_dim(
-                piece_values, step_index * step_rows, step_rows, 0
-            )
-            key_block = key_block.reshape(step_rows, HEADS, HEAD)
-            value_block = value_block.reshape(step_rows, HEADS, HEAD)
-            scores = (
-                jnp.einsum(
-                    "qhd,khd->hqk", query_heads, key_block, preferred_element_type=jnp.float32
-                )
-                * 0.125
-            )
-            key_index = first_key + jnp.arange(step_rows, dtype=jnp.int32)
-            allowed = (key_index[None, :] <= query_index[:, None])[None]
-            scores = jnp.where(allowed, scores, -1e30)
-            new_peak = jnp.maximum(run_peak, jnp.max(scores, axis=-1))
-            weights = jnp.where(allowed, jnp.exp(scores - new_peak[..., None]), 0.0)
-            rescale = jnp.exp(run_peak - new_peak)
-            run_total = run_total * rescale + jnp.sum(weights, axis=-1)
-            weighted = weighted * rescale[..., None] + jnp.einsum(
-                "hqk,khd->hqd",
-                weights.astype(jnp.bfloat16),
-                value_block,
-                preferred_element_type=jnp.float32,
-            )
-            return (new_peak, run_total, weighted)
-
-        return lax.cond(first_key < query_limit, attend, lambda running_in: running_in, running)
-
-    run_peak, run_total, weighted = lax.fori_loop(
-        0, piece_keys.shape[0] // step_rows, one_step, start_state
-    )
-    attended = (weighted / run_total[..., None]).transpose(1, 0, 2).reshape(row_count, D)
-    log_sum = run_peak + jnp.log(run_total)
-    att_low = attended.astype(jnp.bfloat16)
+    _, norm_back_one = jax.vjp(layer_norm, local_frames, first_gain, first_shift)
+    clip_total = lax.axis_size("clip")
+    devices = clip_total * block_total
+    head_width = D // block_total
+    own_weight = jnp.concatenate(
+        [
+            lax.dynamic_slice_in_dim(matrix, block_rank * head_width, head_width, 1)
+            for matrix in (self_query, self_key, self_value)
+        ],
+        axis=1,
+    )
+    att_parts, act_all, qkv, att_full, log_sums = attention_forward(
+        frames[0], own_weight, first_gain[None], first_shift[None], block_total
+    )
+    att_low = att_parts.transpose(1, 0, 2).reshape(row_count, D)
     after_self = local_frames + project(att_low, self_out)
     normed_two, norm_back_two = jax.vjp(layer_norm, after_self, second_gain, second_shift)
     act_two = normed_two.astype(jnp.bfloat16)
@@ -427,90 +750,10 @@
     grad_one_low = grad_one.astype(jnp.bfloat16)
     self_out_term = weight_term(att_low, grad_one_low)
     att_grad = back_project(grad_one_low, self_out).astype(jnp.bfloat16)
-    grad_heads = att_grad.reshape(row_count, HEADS, HEAD)
-    delta_rows = jnp.sum(
-        (att_grad.astype(jnp.float32) * attended).reshape(row_count, HEADS, HEAD), axis=-1
-    ).T
-
-    def block_terms(held_keys, held_values, source_block):
-        key_block = held_keys.reshape(row_count, HEADS, HEAD)
-        value_block = held_values.reshape(row_count, HEADS, HEAD)
-        key_index = source_block * row_count + jnp.arange(row_count, dtype=jnp.int32)
-        allowed = (key_index[None, :] <= query_index[:, None])[None]
-        scores = (
-            jnp.einsum("qhd,khd->hqk", query_heads, key_block, preferred_element_type=jnp.float32)
-            * 0.125
-        )
-        scores = jnp.where(allowed, scores, -1e30)
-        probs = jnp.where(allowed, jnp.exp(scores - log_sum[..., None]), 0.0)
-        dprobs = jnp.einsum(
-            "qhd,khd->hqk", grad_heads, value_block, preferred_element_type=jnp.float32
-        )
-        dscores = (probs * (dprobs - delta_rows[..., None])).astype(jnp.bfloat16)
-        query_term = (
-            jnp.einsum("hqk,khd->hqd", dscores, key_block, preferred_element_type=jnp.float32)
-            * 0.125
-        )
-        key_term = (
-            jnp.einsum(
-                "hqk,qhd->khd", dscores, query_heads, preferred_element_type=jnp.float32
-            ).reshape(row_count, D)
-            * 0.125
-        )
-        value_term = jnp.einsum(
-            "hqk,qhd->khd",
-            probs.astype(jnp.bfloat16),
-            grad_heads,
-            preferred_element_type=jnp.float32,
-        ).reshape(row_count, D)
-        return (key_term, value_term, query_term)
-
-    def block_grads(held_state, source_block):
-
-        def compute(state_in):
-            held_keys, held_values, key_grads, value_grads, query_grads = state_in
-            key_term, value_term, query_term = block_terms(held_keys, held_values, source_block)
-            return (
-                held_keys,
-                held_values,
-                key_grads + key_term,
-                value_grads + value_term,
-                query_grads + query_term,
-            )
-
-        return lax.cond(source_block <= block_rank, compute, lambda state_in: state_in, held_state)
-
-    def pass_grads(held_state):
-        held_keys, held_values, key_grads, value_grads, query_grads = held_state
-        key_grads, value_grads = (
-            shifted(key_grads.astype(jnp.bfloat16), "blk", 1).astype(key_grads.dtype),
-            shifted(value_grads.astype(jnp.bfloat16), "blk", 1).astype(value_grads.dtype),
-        )
-        return (held_keys, held_values, key_grads, value_grads, query_grads)
-
-    def block_turn(turn, held_state):
-        held_state = block_grads(held_state, (block_rank - turn) % block_total)
-        held_keys, held_values, key_grads, value_grads, query_grads = pass_grads(held_state)
-        held_keys, held_values = shifted_2((held_keys, held_values), "blk", 1)
-        return (held_keys, held_values, key_grads, value_grads, query_grads)
-
-    held_state = (
-        keys_local,
-        values_local,
-        jnp.zeros((row_count, D), jnp.float32),
-        jnp.zeros((row_count, D), jnp.float32),
-        jnp.zeros((HEADS, row_count, HEAD), jnp.float32),
-    )
-    held_state = lax.fori_loop(0, block_total - 1, block_turn, held_state)
-    held_state = block_grads(held_state, (block_rank + 1) % block_total)
-    held_state = pass_grads(held_state)
-    key_grads, value_grads, query_grads = (held_state[2], held_state[3], held_state[4])
-    query_low = query_grads.transpose(1, 0, 2).reshape(row_count, D).astype(jnp.bfloat16)
-    key_low = key_grads.astype(jnp.bfloat16)
-    value_low = value_grads.astype(jnp.bfloat16)
-    self_query_term = weight_term(act_one, query_low)
-    self_key_term = weight_term(act_one, key_low)
-    self_value_term = weight_term(act_one, value_low)
+    grad_parts = att_grad.reshape(row_count, block_total, head_width).transpose(1, 0, 2)
+    own_grads, head_weight = attention_backward(grad_parts, qkv, att_full, log_sums, act_all)
+    own_grads = own_grads.reshape(block_total, row_count, 3, head_width).transpose(2, 1, 0, 3)
+    query_low, key_low, value_low = own_grads.reshape(3, row_count, D)
     grad_act_one = (
         back_project(query_low, self_query)
         + back_project(key_low, self_key)
@@ -518,20 +761,18 @@
     )
     grad_norm_one, first_gain_term, first_shift_term = norm_back_one(grad_act_one)
     frames_grad = (grad_one + grad_norm_one)[None]
-    clip_total = lax.axis_size("clip")
-    devices = clip_total * block_total
-    matrices = [
-        self_query_term, self_key_term, self_value_term, self_out_term, cross_query_term, cross_key_term, cross_value_term, cross_out_term,
-        hidden_in_term, hidden_out_term,
-    ]
+    matrices = [self_out_term, cross_query_term, cross_key_term, cross_value_term, cross_out_term, hidden_in_term, hidden_out_term]
     matrices = [m.astype(jnp.bfloat16).reshape(devices, m.shape[0] // devices, m.shape[1]) for m in matrices]
-    kinds = [(1, 9, j) for j in range(4)] + [(0, 8, j) for j in range(4)] + [(0, j, 0) for j in range(8)]
+    kinds = [(1, 6, j) for j in range(4)] + [(0, 5, j) for j in range(4)] + [(0, j, 0) for j in range(5)]
     vectors = [first_gain_term, first_shift_term, second_gain_term, second_shift_term, third_gain_term, third_shift_term]
     stacked = jnp.stack(vectors + [jnp.zeros_like(first_gain_term)] * 2)
-    *summed, vec_sum = reduce_scatter(matrices, kinds, stacked, clip_total, block_total)
     own = D // devices
+    *matrix_sums, vec_sum, head_sums = reduce_scatter(
+        head_weight.reshape(devices, own, 3 * head_width), matrices, kinds, stacked, clip_total, block_total
+    )
     vec_own = lax.dynamic_slice_in_dim(vec_sum, (lax.axis_index("clip") * block_total + block_rank) * own, own, 1)
-    summed = list(summed) + [vec_own[j] for j in range(6)]
+    head_sums = head_sums.reshape(block_total, own, 3, head_width).transpose(2, 1, 0, 3).reshape(3, own, D).astype(jnp.float32)
+    summed = [head_sums[j] for j in range(3)] + list(matrix_sums) + [vec_own[j] for j in range(6)]
     return (
         output_frames,
         frames_grad,

time: 787 us -> 511 us (0.65)
  starting transfers between devices: 190 us -> 0.33 us
  Pallas kernels: 196 us -> 328 us
  waiting for transfers between devices: 123 us -> 0.04 us
  other arithmetic: 56.8 us -> 4.94 us
  local copies, waits for them, and re-layouts: 65.8 us -> 46.4 us
  matrix products: 127 us -> 108 us
    ppermute x30 -> x0, starting transfers between devices: 189 us -> none  [the longest x14 102 us: shifted_2(): return lax.ppermute(block, axis, route)]
    pallas_call x0 -> x2, Pallas kernels: none -> 141 us  [the longest x1 81.8 us: attention_forward(): pl.pallas_call(forward_kernel, out_shape=[jax.ShapeDtypeStruct((blks, row...]
    all_gather x2 -> x0, waiting for transfers between devices: 69.3 us -> none  [the longest x1 41.5 us: body(): piece_keys = lax.all_gather(keys_local, 'blk', axis=0, tiled=True)]
    convert_element_type x31 -> x0, other arithmetic: 32.3 us -> none  [the longest x8 8.14 us: pass_grads(): value_grads.astype(jnp.bfloat16)]
    ppermute x30 -> x0, waiting for transfers between devices: 30 us -> none  [the longest x16 29.9 us: shifted(): return lax.ppermute(block, axis, route)]
    unnamed x6 -> x4, waiting for transfers between devices: 23.3 us -> 0.04 us
    while x14 -> x0, local copies, waits for them, and re-layouts: 13.3 us -> none
    while x7 -> x0, other arithmetic: 10.3 us -> none
  transfers between devices with their start and end apart: 34 -> 2, of which waited for: 7 -> 0; matrix products, arithmetic and copies ran while one was open for 18% -> 11% of each run, Pallas kernels for 0% -> 12%
where the time goes in v2:
time: 511 us; the launch traced here: 504 us
  Pallas kernels  328 us (64%)
  matrix products  108 us (21%)
  local copies, waits for them, and re-layouts  46.4 us (9%)
  between operations  15.6 us (3%)
    pallas_call x1, Pallas kernels, reduce_scatter(): pl.pallas_call(partial(scatter_kernel, clips, blks, kinds), out_shape=[ja...  188 us
    pallas_call x1, Pallas kernels, attention_forward(): pl.pallas_call(forward_kernel, out_shape=[jax.ShapeDtypeStruct((blks, row...  81.8 us
    pallas_call x1, Pallas kernels, attention_backward(): pl.pallas_call(backward_kernel, out_shape=[jax.ShapeDtypeStruct((blks, ro...  58.8 us
    dot_general x7, matrix products, project(): return jnp.dot(left, right, preferred_element_type=jnp.float32)  33.3 us
    dot_general x10, matrix products, back_project(): jnp.einsum('te,de->td', left, right, preferred_element_type=jnp.float32)  30.4 us
    unnamed x120, local copies, waits for them, and re-layouts  26.7 us
    dot_general x7, matrix products, weight_term(): jnp.einsum('td,te->de', left, right, preferred_element_type=jnp.float32)  25.2 us
  transfers between devices with their start and end apart: 2, of which 0 were waited for; matrix products, arithmetic and copies ran while one was open for 11% of the time, Pallas kernels for 12%

profile of v2, /device:TPU:0, one launch (start us, length us, event | category | flops | bytes accessed | tf_op | source)
XLA Modules:
  0.0 503.6 jit_solution(13234172884627907507)
XLA Ops:
  12.0 81.8 %shard_map.339 = (bf16[8,256,128]{2,1,0:T(8,128)(2,1)S(1)}, bf16[8,256,1024]{2,1,0:T(8,128)(2,1)}, bf16[8,256,384]{2,1,0:T(8,128)(2,1)S(1)}, f32[8,256,128]{2,1,0:T(8,128)S(1)}, f32[8,256,128]{2,1,0:T(8,128)S(1)}) custom-call(bf16[256,1024]{1,0:T(8,128)(2,1)S(1)} %bitcast.158, bf16[1024,384]{1,0:T(8,128)(2,1)S(1)} %pad_maximum_fusion.weight, ...), custom_call_target="tpu_custom_call" | custom-call | tf_op jit(solution)/shard_map/pallas_call | solution.py:463
  98.0 3.3 convolution_convert_fusion.13
  104.0 2.4 fusion.57
  109.2 3.3 convolution_convert_fusion.11
  113.7 4.8 fusion.58
  118.6 3.0 convolution_convert_fusion.10
  123.0 15.4 %multiply_convert_fusion.1 = (bf16[256,4096]{1,0:T(8,128)(2,1)}, f32[256,4096]{1,0:T(8,128)S(1)}, f32[256,4096]{1,0:T(8,128)}) fusion(bf16[1024,4096]{1,0:T(8,128)(2,1)} %param.32, f32[256,1024]{1,0:T(8,128)S(1)} %get-tuple-element.87, f32[1024]{0:T(1024)S(1)} %copy-done.50, f32[1024]{0:T(1024)S(1)} %copy-done.49, f32[256]{0:T(256)S(1)} %fusion.45, ...), kind=kOutput, calls=%fused_computation.8 | convolution fusion | flops 2216951808 | bytes 19933184 | tf_op jit(solution)/shard_map/dot_general | solution.py:608
  138.4 10.9 %add_convert_fusion = bf16[256,4096]{1,0:T(8,128)(2,1)S(1)} fusion(f32[256,4096]{1,0:T(8,128)S(1)} %get-tuple-element.67, f32[256,4096]{1,0:T(8,128)} %get-tuple-element.88, bf16[4096,1024]{1,0:T(8,128)(2,1)} %param.33, bf16[1,256,1024]{2,1,0:T(8,128)(2,1)S(1)} %copy-done.24), kind=kOutput, calls=%fused_computation.7 | convolution fusion | flops 2162163712 | bytes 19398656 | tf_op jit(solution)/shard_map/te,de->td/dot_general | solution.py:616
  149.4 6.8 %multiply_reduce_fusion.1 = (f32[1024]{0:T(1024)S(1)}, f32[256]{0:T(256)S(1)}, f32[1024]{0:T(1024)S(1)}, f32[256,1024]{1,0:T(8,128)S(1)}) fusion(f32[256,1024]{1,0:T(8,128)S(1)} %get-tuple-element.87, f32[256]{0:T(256)S(1)} %fusion.45, f32[256]{0:T(256)S(1)} %broadcast_multiply_fusion.1, f32[1024]{0:T(1024)S(1)} %copy-done.49, ...), kind=kOutput, calls=%fused_computation.67 | convolution fusion | flops 2149578496 | bytes 12598272 | tf_op jit(solution)/shard_map/te,de->td/dot_general | solution.py:616
  162.2 3.5 multiply_reduce_fusion
  172.2 3.9 convolution_convert_fusion.7
  178.2 2.3 fusion.16
  180.7 2.4 multiply_reduce_fusion.2
  187.7 2.2 convolution_convert_fusion.5
  192.0 5.7 %convolution_convert_fusion.1 = bf16[1024,4096]{1,0:T(8,128)(2,1)} fusion(bf16[256,4096]{1,0:T(8,128)(2,1)S(1)} %copy-done.31, f32[256,1024]{1,0:T(8,128)S(1)} %copy-done.17, f32[1024]{0:T(1024)S(1)} %copy-done.50, f32[1024]{0:T(1024)S(1)} %copy-done.49, f32[256]{0:T(256)S(1)} %fusion.45, f32[256]{0:T(256)S(1)} %broadcast_multiply_fusion.1), kind=kOutput, calls=%fused_computation.2 | convolution fusion | flops 2152988672 | bytes 11544576 | tf_op jit(solution)/shard_map/td,te->de/dot_general | solution.py:612
  202.5 58.8 %shard_map.340 = (bf16[8,256,384]{2,1,0:T(8,128)(2,1)S(1)}, bf16[1024,384]{1,0:T(8,128)(2,1)S(1)}) custom-call(bf16[8,256,128]{2,1,0:T(8,128)(2,1)S(1)} %bitcast.159, bf16[8,256,384]{2,1,0:T(8,128)(2,1)} %copy-done.3, f32[8,256,128]{2,1,0:T(8,128)S(1)} %copy-done.6, f32[8,256,128]{2,1,0:T(8,128)S(1)} %copy-done.8, bf16[8,256,1024]{2,1,0:T(8,128)(2,1)} %get-tuple-element.39.act), custom_call_target="tpu_custom_call" | custom-call | tf_op jit(solution)/shard_map/pallas_call | solution.py:582
  263.4 2.6 copy.90
  267.6 2.5 fusion.60
  274.0 7.2 %convolution_convert_fusion = bf16[4096,1024]{1,0:T(8,128)(2,1)} fusion(bf16[256,4096]{1,0:T(8,128)(2,1)} %get-tuple-element.66, bf16[1,256,1024]{2,1,0:T(8,128)(2,1)S(1)} %copy-done.25), kind=kOutput, calls=%fused_computation.1 | convolution fusion | flops 2151677952 | bytes 11010048 | tf_op jit(solution)/shard_map/td,te->de/dot_general | solution.py:612
  281.9 7.3 %fusion.18 = bf16[1,256,1024]{2,1,0:T(8,128)(2,1)} fusion(f32[256,1024]{1,0:T(8,128)} %copy-done.16, bf16[256,4096]{1,0:T(8,128)(2,1)} %get-tuple-element.66, bf16[4096,1024]{1,0:T(8,128)(2,1)} %param.33), kind=kOutput, calls=%fused_computation.60 | convolution fusion | flops 2148007936 | bytes 12058624 | tf_op jit(solution)/shard_map/dot_general | solution.py:608
  289.2 2.9 convolution_convert_fusion.4
  292.1 3.0 convolution_convert_fusion.3
  295.1 187.7 %shard_map.341 = (f32[32,1024]{1,0:T(8,128)}, f32[32,1024]{1,0:T(8,128)}, f32[32,1024]{1,0:T(8,128)}, f32[32,1024]{1,0:T(8,128)}, f32[32,1024]{1,0:T(8,128)}, /*...) custom-call(bf16[32,32,384]{2,1,0:T(8,128)(2,1)} %bitcast.160, ...), custom_call_target="tpu_custom_call" | custom-call | tf_op jit(solution)/shard_map/pallas_call | solution.py:254
  488.0 2.3 fusion.61
  (178 shorter events, 61.9 us)
Async XLA Ops:
  7.2 100.2 %copy-start = (bf16[1024,1024]{1,0:T(8,128)(2,1)S(1)}, bf16[1024,1024]{1,0:T(8,128)(2,1)}, u32[]{:S(2)}) copy-start(bf16[1024,1024]{1,0:T(8,128)(2,1)} %param.28) | copy-start | bytes 6291460
  7.2 282.0 %reduce-scatter.7.cloned.1.call-start = ((), (), s32[]{:S(2)}) async-start(), calls=%async_computation.2 | async-start | bytes 589824
  9.5 94.5 %copy-start.2 = (bf16[1,256,1024]{2,1,0:T(8,128)(2,1)S(1)}, bf16[1,256,1024]{2,1,0:T(8,128)(2,1)}, u32[]{:S(2)}) copy-start(bf16[1,256,1024]{2,1,0:T(8,128)(2,1)} %param.20) | copy-start | bytes 1572868
  98.0 6.0 %copy-start.26 = (bf16[256,8,128]{0,2,1:T(8,128)(2,1)S(1)}, bf16[256,8,128]{0,2,1:T(8,128)(2,1)}, u32[]{:S(2)}) copy-start(bf16[256,8,128]{0,2,1:T(8,128)(2,1)} %copy.81) | copy-start | bytes 1572868
  98.0 9.4 %copy-start.52 = (f32[1024]{0:T(1024)S(1)}, f32[1024]{0:T(1024)}, u32[]{:S(2)}) copy-start(f32[1024]{0:T(1024)} %param.36) | copy-start | bytes 12292
  98.0 9.4 %copy-start.53 = (f32[1024]{0:T(1024)S(1)}, f32[1024]{0:T(1024)}, u32[]{:S(2)}) copy-start(f32[1024]{0:T(1024)} %param.37) | copy-start | bytes 12292
  113.7 7.8 %copy-start.36 = (bf16[256,1024]{0,1:T(8,128)(2,1)}, bf16[256,1024]{0,1:T(8,128)(2,1)S(1)}, u32[]{:S(2)}) copy-start(bf16[256,1024]{0,1:T(8,128)(2,1)S(1)} %copy.84) | copy-start | bytes 1572868
  121.6 16.9 %copy-start.34 = (bf16[16,64,256]{2,1,0:T(8,128)(2,1)}, bf16[16,64,256]{2,1,0:T(8,128)(2,1)S(1)}, u32[]{:S(2)}) copy-start(bf16[16,64,256]{2,1,0:T(8,128)(2,1)S(1)} %convolution_convert_fusion.10) | copy-start | bytes 1572868
  122.7 33.5 %copy-start.16 = (f32[256,1024]{1,0:T(8,128)}, f32[256,1024]{1,0:T(8,128)S(1)}, u32[]{:S(2)}) copy-start(f32[256,1024]{1,0:T(8,128)S(1)} %get-tuple-element.87) | copy-start | bytes 3145732
  123.0 15.4 %copy-start.24 = (bf16[1,256,1024]{2,1,0:T(8,128)(2,1)S(1)}, bf16[1,256,1024]{2,1,0:T(8,128)(2,1)}, u32[]{:S(2)}) copy-start(bf16[1,256,1024]{2,1,0:T(8,128)(2,1)} %param.23) | copy-start | bytes 1572868
  149.4 6.8 %copy-start.30 = (bf16[256,4096]{1,0:T(8,128)(2,1)}, bf16[256,4096]{1,0:T(8,128)(2,1)S(1)}, u32[]{:S(2)}) copy-start(bf16[256,4096]{1,0:T(8,128)(2,1)S(1)} %add_convert_fusion) | copy-start | bytes 6291460
  171.9 120.3 %reduce-scatter.9.cloned.1.call-start = ((), (), s32[]{:S(2)}) async-start(), calls=%async_computation.3 | async-start | bytes 589824
  178.2 4.9 copy-start.15
  187.7 4.3 copy-start.31
  295.1 192.9 %copy-start.42 = (bf16[32,1024]{1,0:T(8,128)(2,1)S(1)}, bf16[32,1024]{1,0:T(8,128)(2,1)}, u32[]{:S(2)}) copy-start(bf16[32,1024]{1,0:T(8,128)(2,1)} %reduce-scatter.7.cloned.1.call-done) | copy-start | bytes 196612
  482.8 7.5 %copy-start.43 = (bf16[32,1024]{1,0:T(8,128)(2,1)S(1)}, bf16[32,1024]{1,0:T(8,128)(2,1)}, u32[]{:S(2)}) copy-start(bf16[32,1024]{1,0:T(8,128)(2,1)} %reduce-scatter.9.cloned.1.call-done) | copy-start | bytes 196612
  482.8 8.9 %copy-start.48 = (f32[32,1024]{1,0:T(8,128)S(1)}, f32[32,1024]{1,0:T(8,128)}, u32[]{:S(2)}) copy-start(f32[32,1024]{1,0:T(8,128)} %get-tuple-element.121) | copy-start | bytes 393220
  482.9 9.5 %copy-start.47 = (f32[32,1024]{1,0:T(8,128)S(1)}, f32[32,1024]{1,0:T(8,128)}, u32[]{:S(2)}) copy-start(f32[32,1024]{1,0:T(8,128)} %get-tuple-element.122) | copy-start | bytes 393220
  482.9 10.2 %copy-start.46 = (f32[32,1024]{1,0:T(8,128)S(1)}, f32[32,1024]{1,0:T(8,128)}, u32[]{:S(2)}) copy-start(f32[32,1024]{1,0:T(8,128)} %get-tuple-element.123) | copy-start | bytes 393220
  482.9 10.8 %copy-start.45 = (f32[32,1024]{1,0:T(8,128)S(1)}, f32[32,1024]{1,0:T(8,128)}, u32[]{:S(2)}) copy-start(f32[32,1024]{1,0:T(8,128)} %get-tuple-element.124) | copy-start | bytes 393220
  484.0 6.3 %copy-start.33 = (bf16[1024,1024]{1,0:T(8,128)(2,1)S(1)}, bf16[1024,1024]{1,0:T(8,128)(2,1)}, u32[]{:S(2)}) copy-start(bf16[1024,1024]{1,0:T(8,128)(2,1)} %param.30) | copy-start | bytes 6291460
  484.0 10.3 %copy-start.44 = (f32[32,1024]{1,0:T(8,128)S(1)}, f32[32,1024]{1,0:T(8,128)}, u32[]{:S(2)}) copy-start(f32[32,1024]{1,0:T(8,128)} %get-tuple-element.125) | copy-start | bytes 393220
  484.1 10.9 %copy-start.41 = (f32[32,4096]{1,0:T(8,128)S(1)}, f32[32,4096]{1,0:T(8,128)}, u32[]{:S(2)}) copy-start(f32[32,4096]{1,0:T(8,128)} %get-tuple-element.126) | copy-start | bytes 1572868
  484.5 11.3 %copy-start.40 = (f32[128,1024]{1,0:T(8,128)S(1)}, f32[128,1024]{1,0:T(8,128)}, u32[]{:S(2)}) copy-start(f32[128,1024]{1,0:T(8,128)} %get-tuple-element.127) | copy-start | bytes 1572868
  (32 other events, 65.4 us)
Sparse Core Ops, SparseCore 0:
  172.0 32.7 reduce-scatter.6
  207.2 37.4 reduce-scatter.8
